TPU v7x, 32 devices: a whole 2x2x4 slice. The times are simulated.
32 devices in a mesh: rep: 2 (over core), own: 16 (over z, y, x).
Axes of the slice: x: 2, y: 2, z: 4, core: 2. Of those that a mesh axis runs over, the one named last changes fastest.
Arguments:
- weights: float32 [512, 8, 4096], P('own'), may hold values from -6 to 6
- differences: float32 [2, 512, 8, 4096], P('rep', 'own'), may hold values from -6 to 6
- bases: float32 [6, 4096, 64], replicated, may hold values from -0.09375 to 0.09375
- momentum: float32 [16, 16, 4, 8, 64], P('own'), may hold values from -6 to 6
- owners: int32 [512, 1], replicated, may hold values from 0 to 15; in each aligned block of 32 rows (0 to 31, 32 to 63, ...) at most 4 rows name the same one
- matrix_ids: int32 [512], replicated, may hold values from 0 to 5, never falling along the last dimension, each value on 1 to 127 neighbouring positions
Outputs:
- new_weights: float32 [512, 8, 4096], P('own')
- new_momentum: float32 [16, 16, 4, 8, 64], P('own')
Inputs may be any that keep to these rules, and one draw needn't show every extreme that they name: `owners`: the 32 slabs of one holder name each owner at most 4 times, a bound that some block reaches. `matrix_ids`: never falling; each matrix has 1 to 127 slabs, one exactly that many.
All inputs are finite; a program needn't handle non-finite values.
Results may differ from a plain program's by a relative error of at most 0.0001.
Values sent between devices are 32-bit elements; how exact they have to be, the bound alone decides.
No kernel may reach another device: no remote copies, remote signals or barrier semaphores. Data moves between devices by JAX's collectives and lax.ppermute only.
A program may use at most 192 MiB of HBM per device.

v0:
```python
import jax
import jax.numpy as jnp
from jax import lax
from jax.experimental import pallas as pl
from jax.experimental.pallas import tpu as pltpu
from jax.sharding import PartitionSpec as P

outer_rate = 0.7
decay_rate = 0.9
CHUNKS = 4
VMEM_LIMIT = 20 << 20
HOLD_LIMIT = 58 << 20


def split_parts(value):
    high = value.astype(jnp.bfloat16)
    low = (value - high.astype(jnp.float32)).astype(jnp.bfloat16)
    return high, low


def id_span(ids_ref, base, blocks):
    first = ids_ref[base]
    last = ids_ref[base + blocks - 1]
    return first, last


def slabs_upto(ids_ref, base, blocks, index):
    total = jnp.int32(0)
    for k in range(blocks):
        total = total + jnp.where(ids_ref[base + k] <= index, 1, 0)
    return total


def dot_nt(a, b):
    return lax.dot_general(a, b, (((1,), (1,)), ((), ())), preferred_element_type=jnp.float32)


def project_kernel(ids_ref, x_hbm, b_hbm, f_ref, xbuf, bbuf, xhi, xlo, acc, fac, xsem, bsem):
    blocks = x_hbm.shape[0] // 8
    rank = b_hbm.shape[1]
    width = xbuf.shape[2]
    base = lax.axis_index("own") * blocks
    first, last = id_span(ids_ref, base, blocks)
    pairs = (last - first + 2) // 2

    def x_copy(c):
        return pltpu.make_async_copy(
            x_hbm.at[:, pl.ds(c * width, width)], xbuf.at[c], xsem.at[c]
        )

    def b_copy(index, t, c):
        return pltpu.make_async_copy(
            b_hbm.at[index, :, pl.ds(c * width, width)], bbuf.at[t, c], bsem.at[t, c]
        )

    second = jnp.minimum(first + 1, last)
    for c in range(CHUNKS):
        b_copy(first, 0, c).start()
        b_copy(second, 1, c).start()
        x_copy(c).start()

    rows = lax.broadcasted_iota(jnp.int32, fac.shape, 0)

    def pair_step(p, carry):
        m0 = first + 2 * p
        m1 = jnp.minimum(m0 + 1, last)

        @pl.when(p > 0)
        def _():
            for c in range(CHUNKS):
                b_copy(m0, 0, c).start()
                b_copy(m1, 1, c).start()

        for c in range(CHUNKS):
            b_copy(m0, 0, c).wait()
            b_copy(m1, 1, c).wait()

            @pl.when(p == 0)
            def _():
                x_copy(c).wait()
                high, low = split_parts(xbuf[c])
                xhi[c] = high
                xlo[c] = low

            h0, l0 = split_parts(bbuf[0, c])
            h1, l1 = split_parts(bbuf[1, c])
            basis = jnp.concatenate([h0, l0, h1, l1], axis=0)
            part = dot_nt(xhi[c], basis) + dot_nt(xlo[c], basis)
            if c == 0:
                acc[...] = part
            else:
                acc[...] += part
        total = acc[...]
        f0 = total[:, 0:rank] + total[:, rank : 2 * rank]
        f1 = total[:, 2 * rank : 3 * rank] + total[:, 3 * rank : 4 * rank]
        low_edge = 8 * slabs_upto(ids_ref, base, blocks, m0 - 1)
        high_edge = 8 * slabs_upto(ids_ref, base, blocks, m0)
        kept = jnp.where(rows < high_edge, f0, f1)
        fac[...] = jnp.where(rows < low_edge, fac[...], kept)
        return carry

    lax.fori_loop(0, pairs, pair_step, 0)
    half = fac.shape[0] // 2
    f_ref[...] = jnp.concatenate([fac[0:half, :], fac[half : 2 * half, :]], axis=1)


def project_slabs(ids, diff, bases_t):
    rows, width = diff.shape
    rank = bases_t.shape[1]
    chunk = width // CHUNKS
    return pl.pallas_call(
        project_kernel,
        out_shape=jax.ShapeDtypeStruct((rows // 2, 2 * rank), jnp.float32),
        in_specs=[
            pl.BlockSpec(memory_space=pltpu.SMEM),
            pl.BlockSpec(memory_space=pltpu.HBM),
            pl.BlockSpec(memory_space=pltpu.HBM),
        ],
        out_specs=pl.BlockSpec(memory_space=pltpu.VMEM),
        scratch_shapes=[
            pltpu.VMEM((CHUNKS, rows, chunk), jnp.float32),
            pltpu.VMEM((2, CHUNKS, rank, chunk), jnp.float32),
            pltpu.VMEM((CHUNKS, rows, chunk), jnp.bfloat16),
            pltpu.VMEM((CHUNKS, rows, chunk), jnp.bfloat16),
            pltpu.VMEM((rows, 4 * rank), jnp.float32),
            pltpu.VMEM((rows, rank), jnp.float32),
            pltpu.SemaphoreType.DMA((CHUNKS,)),
            pltpu.SemaphoreType.DMA((2, CHUNKS)),
        ],
        compiler_params=pltpu.CompilerParams(vmem_limit_bytes=HOLD_LIMIT),
        cost_estimate=pl.CostEstimate(
            flops=6 * rows * width * rank, bytes_accessed=6 << 20, transcendentals=0
        ),
        name="project_slabs",
    )(ids, diff, bases_t)


def count_ranks(owners_ref, count_ref, base, blocks, visit):
    for n in range(count_ref.shape[0]):
        count_ref[n] = 0
    for k in range(blocks):
        owner = owners_ref[0, base + k]
        rank = count_ref[owner]
        count_ref[owner] = rank + 1
        visit(k, owner, rank)


def pack_kernel(owners_ref, mine_ref, other_ref, mom_ref, out_ref, avg_ref, count_ref):
    n_own, _, lanes = out_ref.shape
    rank = lanes // 2
    blocks = avg_ref.shape[0] // 8
    base = lax.axis_index("own") * blocks
    average = (mine_ref[...] + other_ref[...]) * 0.5
    half = average.shape[0]
    avg_ref[0:half, :] = average[:, 0:rank]
    avg_ref[half : 2 * half, :] = average[:, rank : 2 * rank]
    mom = mom_ref[...].reshape(out_ref.shape[0], out_ref.shape[1], rank)
    out_ref[...] = jnp.concatenate([jnp.zeros_like(mom), mom], axis=2)

    def visit(k, owner, slot):
        out_ref[owner, pl.ds(pl.multiple_of(slot * 8, 8), 8), 0:rank] = avg_ref[8 * k : 8 * k + 8, :]

    count_ranks(owners_ref, count_ref, base, blocks, visit)


def pack_factors(owners, mine, other, momentum):
    n_own, peer, br, rank = momentum.shape
    rows = 2 * mine.shape[0]
    vmem = pl.BlockSpec(memory_space=pltpu.VMEM)
    smem = pl.BlockSpec(memory_space=pltpu.SMEM)
    return pl.pallas_call(
        pack_kernel,
        out_shape=(
            jax.ShapeDtypeStruct((n_own, peer * br, 2 * rank), jnp.float32),
            jax.ShapeDtypeStruct((rows, rank), jnp.float32),
        ),
        in_specs=[smem, vmem, vmem, vmem],
        out_specs=(vmem, vmem),
        scratch_shapes=[pltpu.SMEM((n_own,), jnp.int32)],
        compiler_params=pltpu.CompilerParams(vmem_limit_bytes=4 << 20),
        name="pack_factors",
    )(owners, mine, other, momentum)


def rebuild_kernel(
    ids_ref, owners_ref, recv_ref, avg_ref, mom_ref, w_hbm, b_hbm, nm_ref, out_hbm,
    wbuf, bbuf, lhs, gath, count_ref, wsem, osem, bsem,
):
    rank = lhs.shape[2] // 2
    blocks = avg_ref.shape[0] // 8
    width = wbuf.shape[2]
    base = lax.axis_index("own") * blocks
    first, last = id_span(ids_ref, base, blocks)
    total = last - first + 1

    def w_copy(c):
        return pltpu.make_async_copy(
            w_hbm.at[:, pl.ds(c * width, width)], wbuf.at[c], wsem.at[c]
        )

    def o_copy(c):
        return pltpu.make_async_copy(
            wbuf.at[c], out_hbm.at[:, pl.ds(c * width, width)], osem.at[c]
        )

    def b_copy(t):
        return pltpu.make_async_copy(b_hbm.at[first + t], bbuf.at[t], bsem.at[t])

    for t in range(bbuf.shape[0]):

        @pl.when(t < total)
        def _():
            b_copy(t).start()

    for c in range(CHUNKS):
        w_copy(c).start()

    def visit(k, owner, slot):
        gath[8 * k : 8 * k + 8, :] = recv_ref[owner, pl.ds(pl.multiple_of(slot * 8, 8), 8), :]

    count_ranks(owners_ref, count_ref, base, blocks, visit)
    received = recv_ref[...]
    nm_ref[...] = decay_rate * mom_ref[...] + received[:, :, 0:rank].reshape(mom_ref.shape)
    placed = avg_ref[...]
    held = decay_rate * gath[:, rank : 2 * rank] + placed
    step = -outer_rate * (placed + decay_rate * held)
    rows = lax.broadcasted_iota(jnp.int32, step.shape, 0)
    for t in range(bbuf.shape[0]):

        @pl.when(t < total)
        def _():
            low_edge = 8 * slabs_upto(ids_ref, base, blocks, first + t - 1)
            high_edge = 8 * slabs_upto(ids_ref, base, blocks, first + t)
            chosen = jnp.where((rows >= low_edge) & (rows < high_edge), step, 0.0)
            high, low = split_parts(chosen)
            lhs[t] = jnp.concatenate([high, low], axis=1)
            b_copy(t).wait()

    for c in range(CHUNKS):
        w_copy(c).wait()

        def add_matrix(t, carry):
            high, low = split_parts(bbuf[t, :, pl.ds(c * width, width)])
            basis = jnp.concatenate([high, high, low, low], axis=0)
            left = lhs[t]
            wbuf[c] += jnp.dot(
                jnp.concatenate([left, left], axis=1), basis, preferred_element_type=jnp.float32
            )
            return carry

        lax.fori_loop(0, total, add_matrix, 0)
        o_copy(c).start()
    for c in range(CHUNKS):
        o_copy(c).wait()


def rebuild_slabs(ids, owners, received, average, momentum, weights, bases_t):
    rows, width = weights.shape
    mats, rank, _ = bases_t.shape
    n_own = momentum.shape[0]
    chunk = width // CHUNKS
    vmem = pl.BlockSpec(memory_space=pltpu.VMEM)
    smem = pl.BlockSpec(memory_space=pltpu.SMEM)
    hbm = pl.BlockSpec(memory_space=pltpu.HBM)
    return pl.pallas_call(
        rebuild_kernel,
        out_shape=(
            jax.ShapeDtypeStruct(momentum.shape, jnp.float32),
            jax.ShapeDtypeStruct(weights.shape, jnp.float32),
        ),
        in_specs=[smem, smem, vmem, vmem, vmem, hbm, hbm],
        out_specs=(vmem, hbm),
        scratch_shapes=[
            pltpu.VMEM((CHUNKS, rows, chunk), jnp.float32),
            pltpu.VMEM((mats, rank, width), jnp.float32),
            pltpu.VMEM((mats, rows, 2 * rank), jnp.bfloat16),
            pltpu.VMEM((rows, 2 * rank), jnp.float32),
            pltpu.SMEM((n_own,), jnp.int32),
            pltpu.SemaphoreType.DMA((CHUNKS,)),
            pltpu.SemaphoreType.DMA((CHUNKS,)),
            pltpu.SemaphoreType.DMA((mats,)),
        ],
        compiler_params=pltpu.CompilerParams(vmem_limit_bytes=VMEM_LIMIT),
        cost_estimate=pl.CostEstimate(
            flops=8 * rows * width * rank, bytes_accessed=10 << 20, transcendentals=0
        ),
        name="rebuild_slabs",
    )(ids, owners, received, average, momentum, weights, bases_t)


def per_device(weights, differences, bases, momentum, owners, matrix_ids):
    blocks, br, width = weights.shape
    n_rep = lax.axis_size("rep")
    bases_t = jnp.swapaxes(bases, 1, 2)
    owner_row = owners.T
    mine = project_slabs(matrix_ids, differences.reshape(blocks * br, width), bases_t)
    other = lax.ppermute(mine, "rep", [(i, n_rep - 1 - i) for i in range(n_rep)])
    packed, average = pack_factors(owner_row, mine, other, momentum[0])
    received = lax.all_to_all(packed, "own", split_axis=0, concat_axis=0, tiled=True)
    new_momentum, new_weights = rebuild_slabs(
        matrix_ids, owner_row, received, average, momentum[0],
        weights.reshape(blocks * br, width), bases_t,
    )
    return (new_weights.reshape(weights.shape), new_momentum[None])


def solution(mesh):
    placed = (
        P("own", None, None),
        P("rep", "own", None, None),
        P(),
        P("own", None, None, None, None),
        P(),
        P(),
    )
    return jax.shard_map(
        per_device,
        mesh=mesh,
        in_specs=placed,
        out_specs=(P("own", None, None), P("own", None, None, None, None)),
        check_vma=False,
    )
```

profile of v0, /device:TPU:0, one launch (start us, length us, event | category | flops | bytes accessed | tf_op | source)
XLA Modules:
  0.0 36.4 jit_solution(7820460687753080901)
XLA Ops:
  0.6 0.0 copy-start.2
  0.6 0.0 copy-start.4
  0.7 0.0 copy-start.1
  0.7 0.0 copy-start.5
  0.7 6.8 %project_slabs.1.mine_ref = f32[128,128]{1,0:T(8,128)} custom-call(s32[512]{0:T(512)} %ids_ref.3, f32[256,4096]{1,0:T(8,128)} %bitcast.14, f32[6,64,4096]{2,1,0:T(8,128)} %bitcast.7), custom_call_target="tpu_custom_call" | custom-call | flops 402653184 | bytes 6291456 | tf_op jit(solution)/shard_map/project_slabs/pallas_call | solution.py:111
  7.4 0.5 %collective-permute-start = (f32[128,128]{1,0:T(8,128)}, f32[128,128]{1,0:T(8,128)S(1)}, u32[]{:S(2)}, u32[]{:S(2)}) collective-permute-start(f32[128,128]{1,0:T(8,128)} %project_slabs.1.mine_ref), channel_id=1, source_target_pairs={{0,16},{16,0},{1,17},{17,1},{2,18},{18,2},{3,19},{19,3},{4,20},{20... | collective-permute-start | bytes 196616 | tf_op jit(solution)/shard_map/ppermute | solution.py:297
  7.9 1.1 %collective-permute-done.other_ref = f32[128,128]{1,0:T(8,128)S(1)} collective-permute-done((f32[128,128]{1,0:T(8,128)}, f32[128,128]{1,0:T(8,128)S(1)}, u32[]{:S(2)}, u32[]{:S(2)}) %collective-permute-start) | collective-permute-done | bytes 65568 | tf_op jit(solution)/shard_map/ppermute | solution.py:297
  9.1 0.0 copy-done.2
  9.1 0.0 copy-done.4
  9.1 0.0 copy-start.3
  9.1 0.8 %copy-done.3 = f32[128,128]{1,0:T(8,128)S(1)} copy-done((f32[128,128]{1,0:T(8,128)S(1)}, f32[128,128]{1,0:T(8,128)}, u32[]{:S(2)}) %copy-start.3) | copy-done | bytes 65560
  9.9 0.7 %pack_factors.1 = (f32[16,32,128]{2,1,0:T(8,128)S(1)}, f32[256,64]{1,0:T(8,128)S(1)}) custom-call(s32[1,512]{1,0:T(1,128)S(1)} %bitcast.12, f32[128,128]{1,0:T(8,128)S(1)} %copy-done.3, f32[128,128]{1,0:T(8,128)S(1)} %collective-permute-done.other_ref, f32[16,4,8,64]{3,2,1,0:T(8,128)S(1)} %bitcast.10), custom_call_target="tpu_custom_call" | custom-call | tf_op jit(solution)/shard_map/pack_factors/pallas_call | solution.py:171
  10.7 18.2 %all_to_all.5.recv_ref = f32[16,32,128]{2,1,0:T(8,128)S(1)} all-to-all(f32[16,32,128]{2,1,0:T(8,128)S(1)} %get-tuple-element.6), channel_id=1, replica_groups=mesh['rep'=2,'own'=16] {'own'}, dimensions={0} | all-to-all | bytes 524288 | tf_op jit(solution)/shard_map/all_to_all | solution.py:299
  28.9 0.0 copy-done.1
  28.9 0.0 copy-done.5
  28.9 0.0 copy-start
  28.9 2.8 %copy-done = f32[6,4096,64]{1,2,0:T(8,128)S(1)} copy-done((f32[6,4096,64]{1,2,0:T(8,128)S(1)}, f32[6,4096,64]{1,2,0:T(8,128)}, u32[]{:S(2)}) %copy-start) | copy-done | bytes 6291480
  31.7 4.7 %rebuild_slabs.1 = (f32[16,4,8,64]{3,2,1,0:T(8,128)}, f32[256,4096]{1,0:T(8,128)}) custom-call(s32[512]{0:T(512)S(1)} %copy-done.5, s32[1,512]{1,0:T(1,128)S(1)} %bitcast.13, f32[16,32,128]{2,1,0:T(8,128)S(1)} %all_to_all.5.recv_ref, f32[256,64]{1,0:T(8,128)S(1)} %get-tuple-element.7.avg_ref, f32[16,4,8,64]{3,2,1,0:T(8,128)S(1)} %bitcast.11, ...), custom_call_target="tpu_custom_call" | custom-call | flops 536870912 | bytes 10485760 | tf_op jit(solution)/shard_map/rebuild_slabs/pallas_call | solution.py:265
Async XLA Ops:
  0.6 8.4 %copy-start.2 = (f32[1,16,4,8,64]{4,3,2,1,0:T(8,128)S(1)}, f32[1,16,4,8,64]{4,3,2,1,0:T(8,128)}, u32[]{:S(2)}) copy-start(f32[1,16,4,8,64]{4,3,2,1,0:T(8,128)} %param.9) | copy-start | bytes 393220
  0.6 8.4 %copy-start.4 = (s32[512,1]{0,1:T(1,128)S(1)}, s32[512,1]{0,1:T(1,128)}, u32[]{:S(2)}) copy-start(s32[512,1]{0,1:T(1,128)} %param.10) | copy-start | bytes 6148
  0.7 28.2 %copy-start.1 = (f32[32,8,4096]{2,1,0:T(8,128)S(1)}, f32[32,8,4096]{2,1,0:T(8,128)}, u32[]{:S(2)}) copy-start(f32[32,8,4096]{2,1,0:T(8,128)} %param.6) | copy-start | bytes 12582916
  0.7 28.2 %copy-start.5 = (s32[512]{0:T(512)S(1)}, s32[512]{0:T(512)}, u32[]{:S(2)}) copy-start(s32[512]{0:T(512)} %ids_ref.3) | copy-start | bytes 6148
  7.4 1.6 %collective-permute-start = (f32[128,128]{1,0:T(8,128)}, f32[128,128]{1,0:T(8,128)S(1)}, u32[]{:S(2)}, u32[]{:S(2)}) collective-permute-start(f32[128,128]{1,0:T(8,128)} %project_slabs.1.mine_ref), channel_id=1, source_target_pairs={{0,16},{16,0},{1,17},{17,1},{2,18},{18,2},{3,19},{19,3},{4,20},{20... | collective-permute-start | bytes 196616 | tf_op jit(solution)/shard_map/ppermute | solution.py:297
  9.1 0.8 %copy-start.3 = (f32[128,128]{1,0:T(8,128)S(1)}, f32[128,128]{1,0:T(8,128)}, u32[]{:S(2)}) copy-start(f32[128,128]{1,0:T(8,128)} %project_slabs.1.mine_ref) | copy-start | bytes 196612
  28.9 2.8 %copy-start = (f32[6,4096,64]{1,2,0:T(8,128)S(1)}, f32[6,4096,64]{1,2,0:T(8,128)}, u32[]{:S(2)}) copy-start(f32[6,4096,64]{1,2,0:T(8,128)} %param.8) | copy-start | bytes 18874372
where the time goes:
time: 36.6 us; the launch traced here: 36.4 us
  blocking collectives  18.2 us (50%)
  Pallas kernels  12.2 us (33%)
  local copies, waits for them, and re-layouts  3.64 us (10%)
  waiting for transfers between devices  1.11 us (3%)
  between operations  0.68 us (2%)
  starting transfers between devices  0.52 us (1%)
    all_to_all x1, blocking collectives, per_device(): lax.all_to_all(packed, 'own', split_axis=0, concat_axis=0, tiled=True)  18.2 us
    pallas_call x1, Pallas kernels, project_slabs(): pl.pallas_call(project_kernel, out_shape=jax.ShapeDtypeStruct((rows // 2,...  6.75 us
    pallas_call x1, Pallas kernels, rebuild_slabs(): pl.pallas_call(rebuild_kernel, out_shape=(jax.ShapeDtypeStruct(momentum.s...  4.72 us
    unnamed x12, local copies, waits for them, and re-layouts  3.64 us
    ppermute x1, waiting for transfers between devices, per_device(): lax.ppermute(mine, 'rep', [(i, n_rep - 1 - i) for i in range(n_rep)])  1.11 us
    pallas_call x1, Pallas kernels, pack_factors(): pl.pallas_call(pack_kernel, out_shape=(jax.ShapeDtypeStruct((n_own, peer...  0.75 us
  transfers between devices with their start and end apart: 1, of which 1 were waited for; matrix products, arithmetic and copies ran while one was open for 0% of the time, Pallas kernels for 0%

commit v1 on v0

v1 whole, which is shorter than its diff:
```python
import jax
import jax.numpy as jnp
from jax import lax
from jax.experimental import pallas as pl
from jax.experimental.pallas import tpu as pltpu
from jax.sharding import PartitionSpec as P

outer_rate = 0.7
decay_rate = 0.9
CHUNKS = 4
VMEM_LIMIT = 20 << 20


def split_parts(value):
    high = value.astype(jnp.bfloat16)
    low = (value - high.astype(jnp.float32)).astype(jnp.bfloat16)
    return high, low


def id_span(ids_ref, base, blocks):
    first = ids_ref[base]
    last = ids_ref[base + blocks - 1]
    return first, last


def slabs_upto(ids_ref, base, blocks, index):
    total = jnp.int32(0)
    for k in range(blocks):
        total = total + jnp.where(ids_ref[base + k] <= index, 1, 0)
    return total


def dot_nt(a, b):
    return lax.dot_general(a, b, (((1,), (1,)), ((), ())), preferred_element_type=jnp.float32)


def project_kernel(
    ids_hbm, x_hbm, b_hbm, f_ref, split_ref, ids_ref, xbuf, bbuf, fac, isem, xsem, bsem
):
    blocks = x_hbm.shape[0] // 8
    rank = b_hbm.shape[1]
    base = lax.axis_index("own") * blocks
    ids_copy = pltpu.make_async_copy(ids_hbm, ids_ref, isem)
    x_copy = pltpu.make_async_copy(x_hbm, xbuf, xsem)
    ids_copy.start()
    x_copy.start()

    def b_copy(index, t):
        return pltpu.make_async_copy(b_hbm.at[index], bbuf.at[t], bsem.at[t])

    ids_copy.wait()
    first, last = id_span(ids_ref, base, blocks)
    pairs = (last - first + 2) // 2
    b_copy(first, 0).start()
    b_copy(jnp.minimum(first + 1, last), 1).start()
    x_copy.wait()
    rows = lax.broadcasted_iota(jnp.int32, fac.shape, 0)

    def pair_step(p, carry):
        m0 = first + 2 * p
        m1 = jnp.minimum(m0 + 1, last)
        low_edge = 8 * slabs_upto(ids_ref, base, blocks, m0 - 1)
        high_edge = 8 * slabs_upto(ids_ref, base, blocks, m0)

        @pl.when(p > 0)
        def _():
            b_copy(m0, 0).start()
            b_copy(m1, 1).start()

        b_copy(m0, 0).wait()
        b_copy(m1, 1).wait()
        first_basis = jnp.concatenate(split_parts(bbuf[0]), axis=0)
        second_basis = jnp.concatenate(split_parts(bbuf[1]), axis=0)
        split_ref[2 * p] = first_basis
        split_ref[2 * p + 1] = second_basis
        basis = jnp.concatenate([first_basis, second_basis], axis=0)
        high, low = split_parts(xbuf[...])
        total = dot_nt(high, basis) + dot_nt(low, basis)
        f0 = total[:, 0:rank] + total[:, rank : 2 * rank]
        f1 = total[:, 2 * rank : 3 * rank] + total[:, 3 * rank : 4 * rank]
        kept = jnp.where(rows < high_edge, f0, f1)
        fac[...] = jnp.where(rows < low_edge, fac[...], kept)
        return carry

    lax.fori_loop(0, pairs, pair_step, 0)
    half = fac.shape[0] // 2
    f_ref[...] = jnp.concatenate([fac[0:half, :], fac[half : 2 * half, :]], axis=1)


def project_slabs(ids, diff, bases_t):
    rows, width = diff.shape
    mats, rank, _ = bases_t.shape
    hbm = pl.BlockSpec(memory_space=pltpu.HBM)
    vmem = pl.BlockSpec(memory_space=pltpu.VMEM)
    return pl.pallas_call(
        project_kernel,
        out_shape=(
            jax.ShapeDtypeStruct((rows // 2, 2 * rank), jnp.float32),
            jax.ShapeDtypeStruct((mats + mats % 2, 2 * rank, width), jnp.bfloat16),
        ),
        in_specs=[hbm, hbm, hbm],
        out_specs=(vmem, vmem),
        scratch_shapes=[
            pltpu.SMEM(ids.shape, jnp.int32),
            pltpu.VMEM((rows, width), jnp.float32),
            pltpu.VMEM((2, rank, width), jnp.float32),
            pltpu.VMEM((rows, rank), jnp.float32),
            pltpu.SemaphoreType.DMA,
            pltpu.SemaphoreType.DMA,
            pltpu.SemaphoreType.DMA((2,)),
        ],
        compiler_params=pltpu.CompilerParams(vmem_limit_bytes=VMEM_LIMIT),
        cost_estimate=pl.CostEstimate(
            flops=6 * rows * width * rank, bytes_accessed=6 << 20, transcendentals=0
        ),
        name="project_slabs",
    )(
        pltpu.with_memory_space_constraint(ids, pltpu.HBM),
        pltpu.with_memory_space_constraint(diff, pltpu.HBM),
        pltpu.with_memory_space_constraint(bases_t, pltpu.HBM),
    )


def count_ranks(owners_ref, count_ref, base, blocks, visit):
    for n in range(count_ref.shape[0]):
        count_ref[n] = 0
    for k in range(blocks):
        owner = owners_ref[0, base + k]
        rank = count_ref[owner]
        count_ref[owner] = rank + 1
        visit(k, owner, rank)


def pack_kernel(owners_ref, mine_ref, other_ref, mom_ref, out_ref, avg_ref, count_ref):
    n_own, _, lanes = out_ref.shape
    rank = lanes // 2
    blocks = avg_ref.shape[0] // 8
    base = lax.axis_index("own") * blocks
    average = (mine_ref[...] + other_ref[...]) * 0.5
    half = average.shape[0]
    avg_ref[0:half, :] = average[:, 0:rank]
    avg_ref[half : 2 * half, :] = average[:, rank : 2 * rank]
    mom = mom_ref[...].reshape(out_ref.shape[0], out_ref.shape[1], rank)
    out_ref[...] = jnp.concatenate([jnp.zeros_like(mom), mom], axis=2)

    def visit(k, owner, slot):
        out_ref[owner, pl.ds(pl.multiple_of(slot * 8, 8), 8), 0:rank] = avg_ref[8 * k : 8 * k + 8, :]

    count_ranks(owners_ref, count_ref, base, blocks, visit)


def pack_factors(owners, mine, other, momentum):
    n_own, peer, br, rank = momentum.shape
    rows = 2 * mine.shape[0]
    vmem = pl.BlockSpec(memory_space=pltpu.VMEM)
    smem = pl.BlockSpec(memory_space=pltpu.SMEM)
    return pl.pallas_call(
        pack_kernel,
        out_shape=(
            jax.ShapeDtypeStruct((n_own, peer * br, 2 * rank), jnp.float32),
            jax.ShapeDtypeStruct((rows, rank), jnp.float32),
        ),
        in_specs=[smem, vmem, vmem, vmem],
        out_specs=(vmem, vmem),
        scratch_shapes=[pltpu.SMEM((n_own,), jnp.int32)],
        compiler_params=pltpu.CompilerParams(vmem_limit_bytes=4 << 20),
        name="pack_factors",
    )(owners, mine, other, momentum)


def rebuild_kernel(
    ids_ref, owners_ref, recv_ref, avg_ref, mom_ref, w_ref, split_ref, nm_hbm, out_hbm,
    obuf, nbuf, lhs, gath, count_ref, osem, nsem,
):
    rank = lhs.shape[2] // 2
    blocks = avg_ref.shape[0] // 8
    width = obuf.shape[2]
    base = lax.axis_index("own") * blocks
    first, last = id_span(ids_ref, base, blocks)
    total = last - first + 1

    def o_copy(c):
        return pltpu.make_async_copy(
            obuf.at[c], out_hbm.at[:, pl.ds(c * width, width)], osem.at[c]
        )

    n_copy = pltpu.make_async_copy(nbuf, nm_hbm, nsem)

    def visit(k, owner, slot):
        gath[8 * k : 8 * k + 8, :] = recv_ref[owner, pl.ds(pl.multiple_of(slot * 8, 8), 8), :]

    count_ranks(owners_ref, count_ref, base, blocks, visit)
    placed = avg_ref[...]
    held = decay_rate * gath[:, rank : 2 * rank] + placed
    step = -outer_rate * (placed + decay_rate * held)
    rows = lax.broadcasted_iota(jnp.int32, step.shape, 0)
    for t in range(lhs.shape[0]):

        @pl.when(t < total)
        def _():
            low_edge = 8 * slabs_upto(ids_ref, base, blocks, first + t - 1)
            high_edge = 8 * slabs_upto(ids_ref, base, blocks, first + t)
            chosen = jnp.where((rows >= low_edge) & (rows < high_edge), step, 0.0)
            lhs[t] = jnp.concatenate(split_parts(chosen), axis=1)

    def product(t, c):
        basis = split_ref[t, :, pl.ds(c * width, width)]
        high, low = basis[0:rank], basis[rank : 2 * rank]
        left = lhs[t]
        return jnp.dot(
            jnp.concatenate([left, left], axis=1),
            jnp.concatenate([high, high, low, low], axis=0),
            preferred_element_type=jnp.float32,
        )

    for c in range(CHUNKS):
        obuf[c] = w_ref[:, c * width : (c + 1) * width] + product(0, c)

        def add_matrix(t, carry):
            obuf[c] += product(t, c)
            return carry

        lax.fori_loop(1, total, add_matrix, 0)
        o_copy(c).start()
        if c == 0:
            received = recv_ref[:, :, 0:rank].reshape(mom_ref.shape)
            nbuf[...] = decay_rate * mom_ref[...] + received
            n_copy.start()
    for c in range(CHUNKS):
        o_copy(c).wait()
    n_copy.wait()


def rebuild_slabs(ids, owners, received, average, momentum, weights, split):
    rows, width = weights.shape
    mats, lanes, _ = split.shape
    n_own = momentum.shape[0]
    chunk = width // CHUNKS
    vmem = pl.BlockSpec(memory_space=pltpu.VMEM)
    smem = pl.BlockSpec(memory_space=pltpu.SMEM)
    hbm = pl.BlockSpec(memory_space=pltpu.HBM)
    return pl.pallas_call(
        rebuild_kernel,
        out_shape=(
            jax.ShapeDtypeStruct(momentum.shape, jnp.float32),
            jax.ShapeDtypeStruct(weights.shape, jnp.float32),
        ),
        in_specs=[smem, smem, vmem, vmem, vmem, vmem, vmem],
        out_specs=(hbm, hbm),
        scratch_shapes=[
            pltpu.VMEM((CHUNKS, rows, chunk), jnp.float32),
            pltpu.VMEM(momentum.shape, jnp.float32),
            pltpu.VMEM((mats, rows, lanes), jnp.bfloat16),
            pltpu.VMEM((rows, lanes), jnp.float32),
            pltpu.SMEM((n_own,), jnp.int32),
            pltpu.SemaphoreType.DMA((CHUNKS,)),
            pltpu.SemaphoreType.DMA,
        ],
        compiler_params=pltpu.CompilerParams(vmem_limit_bytes=VMEM_LIMIT),
        cost_estimate=pl.CostEstimate(
            flops=8 * rows * width * lanes, bytes_accessed=8 << 20, transcendentals=0
        ),
        name="rebuild_slabs",
    )(ids, owners, received, average, momentum, weights, split)


def per_device(weights, differences, bases, momentum, owners, matrix_ids):
    blocks, br, width = weights.shape
    n_rep = lax.axis_size("rep")
    bases_t = jnp.swapaxes(bases, 1, 2)
    owner_row = owners.T
    mine, split = project_slabs(matrix_ids, differences.reshape(blocks * br, width), bases_t)
    other = lax.ppermute(mine, "rep", [(i, n_rep - 1 - i) for i in range(n_rep)])
    packed, average = pack_factors(owner_row, mine, other, momentum[0])
    received = lax.all_to_all(packed, "own", split_axis=0, concat_axis=0, tiled=True)
    new_momentum, new_weights = rebuild_slabs(
        matrix_ids, owner_row, received, average, momentum[0],
        weights.reshape(blocks * br, width), split,
    )
    return (new_weights.reshape(weights.shape), new_momentum[None])


def solution(mesh):
    placed = (
        P("own", None, None),
        P("rep", "own", None, None),
        P(),
        P("own", None, None, None, None),
        P(),
        P(),
    )
    return jax.shard_map(
        per_device,
        mesh=mesh,
        in_specs=placed,
        out_specs=(P("own", None, None), P("own", None, None, None, None)),
        check_vma=False,
    )
```

time: 36.6 us -> 30 us (0.82); the launches traced: 36.4 us -> 30.4 us
  local copies, waits for them, and re-layouts: 3.64 us -> 0.02 us
  Pallas kernels: 12.2 us -> 10.1 us
    unnamed x12 -> x8, local copies, waits for them, and re-layouts: 3.64 us -> 0.02 us
    pallas_call x1, Pallas kernels: 6.75 us -> 4.61 us  [project_slabs(): pl.pallas_call(project_kernel, out_shape=(jax.ShapeDtypeStruct((rows // 2...]
where the time goes in v1:
time: 30 us; the launch traced here: 30.4 us
  blocking collectives  18.2 us (61%)
  Pallas kernels  10.1 us (34%)
  waiting for transfers between devices  0.9 us (3%)
  between operations  0.68 us (2%)
  starting transfers between devices  0.52 us (2%)
    all_to_all x1, blocking collectives, per_device(): lax.all_to_all(packed, 'own', split_axis=0, concat_axis=0, tiled=True)  18.2 us
    pallas_call x1, Pallas kernels, rebuild_slabs(): pl.pallas_call(rebuild_kernel, out_shape=(jax.ShapeDtypeStruct(momentum.s...  4.7 us
    pallas_call x1, Pallas kernels, project_slabs(): pl.pallas_call(project_kernel, out_shape=(jax.ShapeDtypeStruct((rows // 2...  4.61 us
    ppermute x1, waiting for transfers between devices, per_device(): lax.ppermute(mine, 'rep', [(i, n_rep - 1 - i) for i in range(n_rep)])  0.9 us
    pallas_call x1, Pallas kernels, pack_factors(): pl.pallas_call(pack_kernel, out_shape=(jax.ShapeDtypeStruct((n_own, peer...  0.75 us
  transfers between devices with their start and end apart: 1, of which 1 were waited for; matrix products, arithmetic and copies ran while one was open for 0% of the time, Pallas kernels for 0%

profile of v1, /device:TPU:0, one launch (start us, length us, event | category | flops | bytes accessed | tf_op | source)
XLA Modules:
  0.0 30.4 jit_solution(11267110779903046851)
XLA Ops:
  0.6 0.0 copy-start.1
  0.6 0.0 copy-start.2
  0.7 0.0 copy-start
  0.7 0.0 copy-start.3
  0.7 4.6 %project_slabs.1 = (f32[128,128]{1,0:T(8,128)S(1)}, bf16[6,128,4096]{2,1,0:T(8,128)(2,1)S(1)}) custom-call(s32[512]{0:T(512)} %ids_ref.1, f32[256,4096]{1,0:T(8,128)} %bitcast.13, f32[6,64,4096]{2,1,0:T(8,128)} %bitcast.12), custom_call_target="tpu_custom_call" | custom-call | flops 402653184 | bytes 6291456 | tf_op jit(solution)/shard_map/project_slabs/pallas_call | solution.py:95
  5.3 0.5 %collective-permute-start = (f32[128,128]{1,0:T(8,128)S(1)}, f32[128,128]{1,0:T(8,128)S(1)}, u32[]{:S(2)}, u32[]{:S(2)}) collective-permute-start(f32[128,128]{1,0:T(8,128)S(1)} %get-tuple-element.8.mine_ref), channel_id=1, source_target_pairs={{0,16},{16,0},{1,17},{17,1},{2,18},{18,2},{3,19},{19,3},{4,20},{20... | collective-permute-start | bytes 196616 | tf_op jit(solution)/shard_map/ppermute | solution.py:273
  5.8 0.9 %collective-permute-done.other_ref = f32[128,128]{1,0:T(8,128)S(1)} collective-permute-done((f32[128,128]{1,0:T(8,128)S(1)}, f32[128,128]{1,0:T(8,128)S(1)}, u32[]{:S(2)}, u32[]{:S(2)}) %collective-permute-start) | collective-permute-done | bytes 65568 | tf_op jit(solution)/shard_map/ppermute | solution.py:273
  6.7 0.0 copy-done.1
  6.7 0.0 copy-done.2
  6.7 0.7 %pack_factors.1 = (f32[16,32,128]{2,1,0:T(8,128)S(1)}, f32[256,64]{1,0:T(8,128)S(1)}) custom-call(s32[1,512]{1,0:T(1,128)S(1)} %bitcast.10, f32[128,128]{1,0:T(8,128)S(1)} %get-tuple-element.8.mine_ref, f32[128,128]{1,0:T(8,128)S(1)} %collective-permute-done.other_ref, f32[16,4,8,64]{3,2,1,0:T(8,128)S(1)} %bitcast.8), custom_call_target="tpu_custom_call" | custom-call | tf_op jit(solution)/shard_map/pack_factors/pallas_call | solution.py:157
  7.5 18.2 %all_to_all.5.recv_ref = f32[16,32,128]{2,1,0:T(8,128)S(1)} all-to-all(f32[16,32,128]{2,1,0:T(8,128)S(1)} %get-tuple-element.9), channel_id=1, replica_groups=mesh['rep'=2,'own'=16] {'own'}, dimensions={0} | all-to-all | bytes 524288 | tf_op jit(solution)/shard_map/all_to_all | solution.py:275
  25.7 0.0 copy-done
  25.7 0.0 copy-done.3
  25.7 4.7 %rebuild_slabs.1 = (f32[16,4,8,64]{3,2,1,0:T(8,128)}, f32[256,4096]{1,0:T(8,128)}) custom-call(s32[512]{0:T(512)S(1)} %copy-done.3, s32[1,512]{1,0:T(1,128)S(1)} %bitcast.11, f32[16,32,128]{2,1,0:T(8,128)S(1)} %all_to_all.5.recv_ref, f32[256,64]{1,0:T(8,128)S(1)} %get-tuple-element.10.avg_ref, f32[16,4,8,64]{3,2,1,0:T(8,128)S(1)} %bitcast.9, ...), custom_call_target="tpu_custom_call" | custom-call | flops 1073741824 | bytes 8388608 | tf_op jit(solution)/shard_map/rebuild_slabs/pallas_call | solution.py:242
Async XLA Ops:
  0.6 6.1 %copy-start.1 = (f32[1,16,4,8,64]{4,3,2,1,0:T(8,128)S(1)}, f32[1,16,4,8,64]{4,3,2,1,0:T(8,128)}, u32[]{:S(2)}) copy-start(f32[1,16,4,8,64]{4,3,2,1,0:T(8,128)} %param.9) | copy-start | bytes 393220
  0.6 6.1 %copy-start.2 = (s32[512,1]{0,1:T(1,128)S(1)}, s32[512,1]{0,1:T(1,128)}, u32[]{:S(2)}) copy-start(s32[512,1]{0,1:T(1,128)} %param.10) | copy-start | bytes 6148
  0.7 25.0 %copy-start = (f32[32,8,4096]{2,1,0:T(8,128)S(1)}, f32[32,8,4096]{2,1,0:T(8,128)}, u32[]{:S(2)}) copy-start(f32[32,8,4096]{2,1,0:T(8,128)} %param.6) | copy-start | bytes 12582916
  0.7 25.0 %copy-start.3 = (s32[512]{0:T(512)S(1)}, s32[512]{0:T(512)}, u32[]{:S(2)}) copy-start(s32[512]{0:T(512)} %ids_ref.1) | copy-start | bytes 6148
  5.3 1.4 %collective-permute-start = (f32[128,128]{1,0:T(8,128)S(1)}, f32[128,128]{1,0:T(8,128)S(1)}, u32[]{:S(2)}, u32[]{:S(2)}) collective-permute-start(f32[128,128]{1,0:T(8,128)S(1)} %get-tuple-element.8.mine_ref), channel_id=1, source_target_pairs={{0,16},{16,0},{1,17},{17,1},{2,18},{18,2},{3,19},{19,3},{4,20},{20... | collective-permute-start | bytes 196616 | tf_op jit(solution)/shard_map/ppermute | solution.py:273

commit v2 on v1

v2 whole, which is shorter than its diff:
```python
import jax
import jax.numpy as jnp
from jax import lax
from jax.experimental import pallas as pl
from jax.experimental.pallas import tpu as pltpu
from jax.sharding import PartitionSpec as P

outer_rate = 0.7
decay_rate = 0.9
CHUNKS = 4
VMEM_LIMIT = 20 << 20
BR = 8


def split_parts(value):
    high = value.astype(jnp.bfloat16)
    low = (value - high.astype(jnp.float32)).astype(jnp.bfloat16)
    return high, low


def dot_nt(a, b):
    return lax.dot_general(a, b, (((1,), (1,)), ((), ())), preferred_element_type=jnp.float32)


def upper_half(shape):
    return lax.broadcasted_iota(jnp.int32, shape, len(shape) - 1) >= shape[-1] // 2


def send_plan(peer):
    pairs = (peer + 1) // 2
    return pairs, (pairs + 1) // 2


def scan_slabs(ids_ref, owners_ref, count_ref, edge_ref, base, blocks, visit):
    for n in range(count_ref.shape[0]):
        count_ref[n] = 0
    first = ids_ref[base]
    edge_ref[0] = 0
    for k in range(blocks):
        edge_ref[ids_ref[base + k] - first + 1] = k + 1
        owner = owners_ref[0, base + k]
        rank = count_ref[owner]
        count_ref[owner] = rank + 1
        visit(k, owner, rank)
    return first, ids_ref[base + blocks - 1]


def project_kernel(
    ids_hbm, owners_hbm, x_hbm, b_hbm, mom_hbm, f_ref, send_ref, split_ref,
    ids_ref, owners_ref, owner_of, rank_of, count_ref, edge_ref,
    xbuf, bbuf, mbuf, fac, isem, osem, xsem, bsem, msem,
):
    blocks = x_hbm.shape[0] // BR
    lanes = send_ref.shape[2]
    rank = lanes // 2
    n_own, peer = mom_hbm.shape[:2]
    pairs, share = send_plan(peer)
    base = lax.axis_index("own") * blocks
    ids_copy = pltpu.make_async_copy(ids_hbm, ids_ref, isem)
    owners_copy = pltpu.make_async_copy(owners_hbm, owners_ref, osem)
    x_copy = pltpu.make_async_copy(x_hbm, xbuf, xsem)
    m_copy = pltpu.make_async_copy(mom_hbm, mbuf.at[:, 0:peer], msem)
    ids_copy.start()
    owners_copy.start()
    x_copy.start()

    def b_copy(index, t):
        return pltpu.make_async_copy(b_hbm.at[index], bbuf.at[t], bsem.at[t])

    ids_copy.wait()
    first = ids_ref[base]
    last = ids_ref[base + blocks - 1]
    b_copy(first, 0).start()
    b_copy(jnp.minimum(first + 1, last), 1).start()
    m_copy.start()
    owners_copy.wait()

    def visit(k, owner, slot):
        owner_of[k] = owner
        rank_of[k] = slot

    scan_slabs(ids_ref, owners_ref, count_ref, edge_ref, base, blocks, visit)
    send_ref[:, 0 : BR * pairs, :] = jnp.zeros((n_own, BR * pairs, lanes), jnp.float32)
    if peer % 2:
        mbuf[:, peer] = jnp.zeros((n_own, BR, rank), jnp.float32)
    m_copy.wait()
    start = lax.axis_index("rep") * (pairs - share)
    for i in range(share):
        slot = 2 * (start + i)
        send_ref[:, BR * (pairs + i) : BR * (pairs + i + 1), :] = jnp.concatenate(
            [mbuf[:, slot], mbuf[:, slot + 1]], axis=2
        )
    x_copy.wait()
    rows = lax.broadcasted_iota(jnp.int32, fac.shape, 0)

    def pair_step(p, carry):
        m0 = first + 2 * p
        m1 = jnp.minimum(m0 + 1, last)

        @pl.when(p > 0)
        def _():
            b_copy(m0, 0).start()
            b_copy(m1, 1).start()

        b_copy(m0, 0).wait()
        b_copy(m1, 1).wait()
        first_basis = jnp.concatenate(split_parts(bbuf[0]), axis=0)
        second_basis = jnp.concatenate(split_parts(bbuf[1]), axis=0)
        split_ref[2 * p] = first_basis
        split_ref[2 * p + 1] = second_basis
        basis = jnp.concatenate([first_basis, second_basis], axis=0)
        high, low = split_parts(xbuf[...])
        total = 0.5 * (dot_nt(high, basis) + dot_nt(low, basis))
        both = []
        for part in (total[:, 0:lanes], total[:, lanes : 2 * lanes]):
            both.append(part + pltpu.roll(part, rank, 1))
        kept = jnp.where(rows < BR * edge_ref[2 * p + 1], both[0], both[1])
        fac[...] = jnp.where(rows < BR * edge_ref[2 * p], fac[...], kept)
        return carry

    lax.fori_loop(0, (last - first + 2) // 2, pair_step, 0)
    half = fac.shape[0] // 2
    f_ref[...] = jnp.where(
        upper_half(f_ref.shape), fac[half : 2 * half, :], fac[0:half, :]
    )
    upper = upper_half((BR, lanes)).astype(jnp.int32)
    for k in range(blocks):
        slot = rank_of[k]
        place = pl.ds(pl.multiple_of(lax.shift_right_logical(slot, 1) * BR, BR), BR)
        tile = send_ref[owner_of[k], place, :]
        mine = upper == lax.bitwise_and(slot, 1)
        send_ref[owner_of[k], place, :] = jnp.where(mine, fac[BR * k : BR * (k + 1), :], tile)


def project_slabs(ids, owners, diff, bases_t, momentum):
    rows, width = diff.shape
    mats, rank, _ = bases_t.shape
    n_own, peer = momentum.shape[:2]
    pairs, share = send_plan(peer)
    blocks = rows // BR
    hbm = pl.BlockSpec(memory_space=pltpu.HBM)
    vmem = pl.BlockSpec(memory_space=pltpu.VMEM)
    return pl.pallas_call(
        project_kernel,
        out_shape=(
            jax.ShapeDtypeStruct((rows // 2, 2 * rank), jnp.float32),
            jax.ShapeDtypeStruct((n_own, BR * (pairs + share), 2 * rank), jnp.float32),
            jax.ShapeDtypeStruct((mats + mats % 2, 2 * rank, width), jnp.bfloat16),
        ),
        in_specs=[hbm] * 5,
        out_specs=(vmem, vmem, vmem),
        scratch_shapes=[
            pltpu.SMEM(ids.shape, jnp.int32),
            pltpu.SMEM(owners.shape, jnp.int32),
            pltpu.SMEM((blocks,), jnp.int32),
            pltpu.SMEM((blocks,), jnp.int32),
            pltpu.SMEM((n_own,), jnp.int32),
            pltpu.SMEM((mats + 2,), jnp.int32),
            pltpu.VMEM((rows, width), jnp.float32),
            pltpu.VMEM((2, rank, width), jnp.float32),
            pltpu.VMEM((n_own, 2 * pairs, BR, rank), jnp.float32),
            pltpu.VMEM((rows, 2 * rank), jnp.float32),
            pltpu.SemaphoreType.DMA,
            pltpu.SemaphoreType.DMA,
            pltpu.SemaphoreType.DMA,
            pltpu.SemaphoreType.DMA((2,)),
            pltpu.SemaphoreType.DMA,
        ],
        compiler_params=pltpu.CompilerParams(vmem_limit_bytes=VMEM_LIMIT),
        cost_estimate=pl.CostEstimate(
            flops=6 * rows * width * rank, bytes_accessed=6 << 20, transcendentals=0
        ),
        name="project_slabs",
    )(*[pltpu.with_memory_space_constraint(v, pltpu.HBM) for v in (ids, owners, diff, bases_t, momentum)])


def rebuild_kernel(
    ids_ref, owners_ref, fmine_ref, fother_ref, mine_ref, other_ref, mom_ref, w_ref, split_ref,
    nm_hbm, out_hbm, obuf, nbuf, sent, lhs, gath, count_ref, edge_ref, osem, nsem,
):
    lanes = gath.shape[1]
    rank = lanes // 2
    blocks = gath.shape[0] // BR
    width = obuf.shape[2]
    n_own, peer = mom_ref.shape[:2]
    pairs, share = send_plan(peer)
    base = lax.axis_index("own") * blocks
    rep = lax.axis_index("rep")

    def o_copy(c):
        return pltpu.make_async_copy(
            obuf.at[c], out_hbm.at[:, pl.ds(c * width, width)], osem.at[c]
        )

    n_copy = pltpu.make_async_copy(nbuf, nm_hbm, nsem)
    sent[rep] = mine_ref[:, BR * pairs : BR * (pairs + share), :]
    sent[1 - rep] = other_ref[:, BR * pairs : BR * (pairs + share), :]
    upper = upper_half((BR, lanes)).astype(jnp.int32)

    def visit(k, owner, slot):
        pair = lax.shift_right_logical(slot, 1)
        source = jnp.where(pair < share, 0, 1)
        row = BR * (pair - source * (pairs - share))
        tile = sent[source, owner, pl.ds(pl.multiple_of(row, BR), BR), :]
        gath[BR * k : BR * (k + 1), :] = jnp.where(upper == lax.bitwise_and(slot, 1), tile, 0.0)

    first, last = scan_slabs(ids_ref, owners_ref, count_ref, edge_ref, base, blocks, visit)
    total = last - first + 1
    average = fmine_ref[...] + fother_ref[...]
    turned = pltpu.roll(average, rank, 1)
    above = upper_half(average.shape)
    placed = jnp.concatenate(
        [jnp.where(above, turned, average), jnp.where(above, average, turned)], axis=0
    )
    picked = gath[...]
    held = decay_rate * (picked + pltpu.roll(picked, rank, 1)) + placed
    step = -outer_rate * (placed + decay_rate * held)
    high = step.astype(jnp.bfloat16).astype(jnp.float32)
    parts = jnp.where(upper_half(step.shape), step - high, high)
    rows = lax.broadcasted_iota(jnp.int32, step.shape, 0)
    for t in range(lhs.shape[0]):

        @pl.when(t < total)
        def _():
            inside = (rows >= BR * edge_ref[t]) & (rows < BR * edge_ref[t + 1])
            lhs[t] = jnp.where(inside, parts, 0.0).astype(jnp.bfloat16)

    def product(t, c):
        basis = split_ref[t, :, pl.ds(c * width, width)]
        top, bottom = basis[0:rank], basis[rank : 2 * rank]
        left = lhs[t]
        return jnp.dot(
            jnp.concatenate([left, left], axis=1),
            jnp.concatenate([top, top, bottom, bottom], axis=0),
            preferred_element_type=jnp.float32,
        )

    for c in range(CHUNKS):
        obuf[c] = w_ref[:, c * width : (c + 1) * width] + product(0, c)

        def add_matrix(t, carry):
            obuf[c] += product(t, c)
            return carry

        lax.fori_loop(1, total, add_matrix, 0)
        o_copy(c).start()
        if c == 0:
            arrived = mine_ref[:, 0 : BR * pairs, :] + other_ref[:, 0 : BR * pairs, :]
            for s in range(peer):
                block = arrived[:, BR * (s // 2) : BR * (s // 2 + 1), :]
                lane = rank * (s % 2)
                nbuf[:, s] = decay_rate * mom_ref[:, s] + block[:, :, lane : lane + rank]
            n_copy.start()
    for c in range(CHUNKS):
        o_copy(c).wait()
    n_copy.wait()


def rebuild_slabs(ids, owners, fmine, fother, mine, other, momentum, weights, split):
    rows, width = weights.shape
    mats, lanes, _ = split.shape
    n_own, peer = momentum.shape[:2]
    _, share = send_plan(peer)
    chunk = width // CHUNKS
    vmem = pl.BlockSpec(memory_space=pltpu.VMEM)
    smem = pl.BlockSpec(memory_space=pltpu.SMEM)
    hbm = pl.BlockSpec(memory_space=pltpu.HBM)
    return pl.pallas_call(
        rebuild_kernel,
        out_shape=(
            jax.ShapeDtypeStruct(momentum.shape, jnp.float32),
            jax.ShapeDtypeStruct(weights.shape, jnp.float32),
        ),
        in_specs=[smem, smem] + [vmem] * 7,
        out_specs=(hbm, hbm),
        scratch_shapes=[
            pltpu.VMEM((CHUNKS, rows, chunk), jnp.float32),
            pltpu.VMEM(momentum.shape, jnp.float32),
            pltpu.VMEM((2, n_own, BR * share, lanes), jnp.float32),
            pltpu.VMEM((mats, rows, lanes), jnp.bfloat16),
            pltpu.VMEM((rows, lanes), jnp.float32),
            pltpu.SMEM((n_own,), jnp.int32),
            pltpu.SMEM((mats + 2,), jnp.int32),
            pltpu.SemaphoreType.DMA((CHUNKS,)),
            pltpu.SemaphoreType.DMA,
        ],
        compiler_params=pltpu.CompilerParams(vmem_limit_bytes=VMEM_LIMIT),
        cost_estimate=pl.CostEstimate(
            flops=8 * rows * width * lanes, bytes_accessed=8 << 20, transcendentals=0
        ),
        name="rebuild_slabs",
    )(ids, owners, fmine, fother, mine, other, momentum, weights, split)


def per_device(weights, differences, bases, momentum, owners, matrix_ids):
    blocks, br, width = weights.shape
    swap = [(0, 1), (1, 0)]
    bases_t = jnp.swapaxes(bases, 1, 2)
    owner_row = owners.T
    fmine, packed, split = project_slabs(
        matrix_ids, owner_row, differences.reshape(blocks * br, width), bases_t, momentum[0]
    )
    fother = lax.ppermute(fmine, "rep", swap)
    mine = lax.all_to_all(packed, "own", split_axis=0, concat_axis=0, tiled=True)
    other = lax.ppermute(mine, "rep", swap)
    new_momentum, new_weights = rebuild_slabs(
        matrix_ids, owner_row, fmine, fother, mine, other, momentum[0],
        weights.reshape(blocks * br, width), split,
    )
    return (new_weights.reshape(weights.shape), new_momentum[None])


def solution(mesh):
    placed = (
        P("own", None, None),
        P("rep", "own", None, None),
        P(),
        P("own", None, None, None, None),
        P(),
        P(),
    )
    return jax.shard_map(
        per_device,
        mesh=mesh,
        in_specs=placed,
        out_specs=(P("own", None, None), P("own", None, None, None, None)),
        check_vma=False,
    )
```

time: 30 us -> 27.3 us (0.910); the launches traced: 30.4 us -> 27.1 us
  Pallas kernels: 10.1 us -> 8.15 us
  blocking collectives: 18.2 us -> 16.7 us
    all_to_all x1, blocking collectives: 18.2 us -> 16.7 us  [per_device(): lax.all_to_all(packed, 'own', split_axis=0, concat_axis=0, tiled=True)]
    pallas_call x1, Pallas kernels: 4.7 us -> 3.4 us  [rebuild_slabs(): pl.pallas_call(rebuild_kernel, out_shape=(jax.ShapeDtypeStruct(momentum.s...]
    pallas_call x1 -> x0, Pallas kernels: 0.75 us -> none  [pack_factors(): pl.pallas_call(pack_kernel, out_shape=(jax.ShapeDtypeStruct((n_own, peer...]
    ppermute x1 -> x2, waiting for transfers between devices: 0.9 us -> 1.03 us  [the longest x1 1.02 us: per_device(): fother = lax.ppermute(fmine, 'rep', swap)]
  transfers between devices with their start and end apart: 1 -> 2, of which waited for: 1 -> 1; matrix products, arithmetic and copies ran while one was open for 0% -> 0% of each run, Pallas kernels for 0% -> 0%
where the time goes in v2:
time: 27.3 us; the launch traced here: 27.1 us
  blocking collectives  16.7 us (61%)
  Pallas kernels  8.15 us (30%)
  waiting for transfers between devices  1.03 us (4%)
  between operations  0.69 us (3%)
  starting transfers between devices  0.51 us (2%)
    all_to_all x1, blocking collectives, per_device(): lax.all_to_all(packed, 'own', split_axis=0, concat_axis=0, tiled=True)  16.7 us
    pallas_call x1, Pallas kernels, project_slabs(): pl.pallas_call(project_kernel, out_shape=(jax.ShapeDtypeStruct((rows // 2...  4.75 us
    pallas_call x1, Pallas kernels, rebuild_slabs(): pl.pallas_call(rebuild_kernel, out_shape=(jax.ShapeDtypeStruct(momentum.s...  3.4 us
    ppermute x1, waiting for transfers between devices, per_device(): fother = lax.ppermute(fmine, 'rep', swap)  1.02 us
  transfers between devices with their start and end apart: 2, of which 1 were waited for; matrix products, arithmetic and copies ran while one was open for 0% of the time, Pallas kernels for 0%

profile of v2, /device:TPU:0, one launch (start us, length us, event | category | flops | bytes accessed | tf_op | source)
XLA Modules:
  0.0 27.1 jit_solution(2139688222964551487)
XLA Ops:
  0.6 0.0 copy-start
  0.6 0.0 copy-start.1
  0.7 0.0 copy-start.2
  0.7 0.0 copy-start.3
  0.7 4.8 %project_slabs.1 = (f32[128,128]{1,0:T(8,128)S(1)}, f32[16,24,128]{2,1,0:T(8,128)S(1)}, bf16[6,128,4096]{2,1,0:T(8,128)(2,1)S(1)}) custom-call(s32[512]{0:T(512)} %ids_ref.1, s32[1,512]{1,0:T(1,128)} %bitcast.10, f32[256,4096]{1,0:T(8,128)} %bitcast.13, f32[6,64,4096]{2,1,0:T(8,128)} %bitcast.12, f32[16,4,8,64]{3,2,1,0:T(8,128)} %bitcast.8), custom_call_target="tpu_custom_call" | custom-call | flops 402653184 | bytes 6291456 | tf_op jit(solution)/shard_map/project_slabs/pallas_call | solution.py:143
  5.4 16.7 %all_to_all.5.mine_ref = f32[16,24,128]{2,1,0:T(8,128)S(1)} all-to-all(f32[16,24,128]{2,1,0:T(8,128)S(1)} %get-tuple-element.8), channel_id=1, replica_groups=mesh['rep'=2,'own'=16] {'own'}, dimensions={0} | all-to-all | bytes 393216 | tf_op jit(solution)/shard_map/all_to_all | solution.py:304
  22.2 0.0 collective-permute-start.1
  22.2 0.5 %collective-permute-start = (f32[128,128]{1,0:T(8,128)S(1)}, f32[128,128]{1,0:T(8,128)S(1)}, u32[]{:S(2)}, u32[]{:S(2)}) collective-permute-start(f32[128,128]{1,0:T(8,128)S(1)} %get-tuple-element.7.fmine_ref), channel_id=1, source_target_pairs={{0,16},{16,0},{1,17},{17,1},{2,18},{18,2},{3,19},{19,3},{4,20},{20... | collective-permute-start | bytes 196616 | tf_op jit(solution)/shard_map/ppermute | solution.py:303
  22.7 1.0 %collective-permute-done.fother_ref = f32[128,128]{1,0:T(8,128)S(1)} collective-permute-done((f32[128,128]{1,0:T(8,128)S(1)}, f32[128,128]{1,0:T(8,128)S(1)}, u32[]{:S(2)}, u32[]{:S(2)}) %collective-permute-start) | collective-permute-done | bytes 65568 | tf_op jit(solution)/shard_map/ppermute | solution.py:303
  23.7 0.0 collective-permute-done.1.other_ref
  23.7 0.0 copy-done
  23.7 0.0 copy-done.1
  23.7 0.0 copy-done.2
  23.7 0.0 copy-done.3
  23.8 3.4 %rebuild_slabs.1 = (f32[16,4,8,64]{3,2,1,0:T(8,128)}, f32[256,4096]{1,0:T(8,128)}) custom-call(s32[512]{0:T(512)S(1)} %copy-done.2, s32[1,512]{1,0:T(1,128)S(1)} %bitcast.11, f32[128,128]{1,0:T(8,128)S(1)} %get-tuple-element.7.fmine_ref, f32[128,128]{1,0:T(8,128)S(1)} %collective-permute-done.fother_ref, f32[16,24,128]{2,1,0:T(8,128)S(1)} %all_to_all.5.mine_ref, ...), custom_call_target="tpu_custom_call" | custom-call | flops 1073741824 | bytes 8388608 | tf_op jit(solution)/shard_map/rebuild_slabs/pallas_call | solution.py:268
Async XLA Ops:
  0.6 23.1 %copy-start = (f32[32,8,4096]{2,1,0:T(8,128)S(1)}, f32[32,8,4096]{2,1,0:T(8,128)}, u32[]{:S(2)}) copy-start(f32[32,8,4096]{2,1,0:T(8,128)} %param.6) | copy-start | bytes 12582916
  0.6 23.1 %copy-start.1 = (f32[1,16,4,8,64]{4,3,2,1,0:T(8,128)S(1)}, f32[1,16,4,8,64]{4,3,2,1,0:T(8,128)}, u32[]{:S(2)}) copy-start(f32[1,16,4,8,64]{4,3,2,1,0:T(8,128)} %param.9) | copy-start | bytes 393220
  0.7 23.1 %copy-start.2 = (s32[512]{0:T(512)S(1)}, s32[512]{0:T(512)}, u32[]{:S(2)}) copy-start(s32[512]{0:T(512)} %ids_ref.1) | copy-start | bytes 6148
  0.7 23.1 %copy-start.3 = (s32[512,1]{0,1:T(1,128)S(1)}, s32[512,1]{0,1:T(1,128)}, u32[]{:S(2)}) copy-start(s32[512,1]{0,1:T(1,128)} %param.10) | copy-start | bytes 6148
  22.2 1.5 %collective-permute-start.1 = (f32[16,24,128]{2,1,0:T(8,128)S(1)}, f32[16,24,128]{2,1,0:T(8,128)S(1)}, u32[]{:S(2)}, u32[]{:S(2)}) collective-permute-start(f32[16,24,128]{2,1,0:T(8,128)S(1)} %all_to_all.5.mine_ref), channel_id=1, source_target_pairs={{0,16},{16,0},{1,17},{17,1},{2,18},{18,2},{3,19},{19,3},{4,20},{20... | collective-permute-start | bytes 589832 | tf_op jit(solution)/shard_map/ppermute | solution.py:305
  22.2 1.5 %collective-permute-start = (f32[128,128]{1,0:T(8,128)S(1)}, f32[128,128]{1,0:T(8,128)S(1)}, u32[]{:S(2)}, u32[]{:S(2)}) collective-permute-start(f32[128,128]{1,0:T(8,128)S(1)} %get-tuple-element.7.fmine_ref), channel_id=1, source_target_pairs={{0,16},{16,0},{1,17},{17,1},{2,18},{18,2},{3,19},{19,3},{4,20},{20... | collective-permute-start | bytes 196616 | tf_op jit(solution)/shard_map/ppermute | solution.py:303

commit v3 on v2

v3 whole, which is shorter than its diff:
```python
import jax
import jax.numpy as jnp
from jax import lax
from jax.experimental import pallas as pl
from jax.experimental.pallas import tpu as pltpu
from jax.sharding import PartitionSpec as P

outer_rate = 0.7
decay_rate = 0.9
COLUMNS = (0, 1024, 2048, 3072, 4096)
VMEM_LIMIT = 20 << 20
BR = 8


def split_parts(value):
    high = value.astype(jnp.bfloat16)
    low = (value - high.astype(jnp.float32)).astype(jnp.bfloat16)
    return high, low


def dot_nt(a, b):
    return lax.dot_general(a, b, (((1,), (1,)), ((), ())), preferred_element_type=jnp.float32)


def upper_half(shape):
    return lax.broadcasted_iota(jnp.int32, shape, len(shape) - 1) >= shape[-1] // 2


def send_plan(peer):
    pairs = (peer + 1) // 2
    return pairs, (pairs + 1) // 2


def meta_size(blocks, mats):
    return -(-(blocks + mats + 4) // 128) * 128


def project_kernel(
    ids_hbm, owners_hbm, x_hbm, b_hbm, mom_hbm, f_ref, send_ref, split_ref, meta_hbm,
    ids_ref, owners_ref, owner_of, rank_of, count_ref, meta_ref,
    xbuf, bbuf, mbuf, fac, isem, osem, xsem, bsem, msem, tsem,
):
    blocks = x_hbm.shape[0] // BR
    lanes = send_ref.shape[2]
    rank = lanes // 2
    n_own, peer = mom_hbm.shape[:2]
    pairs, share = send_plan(peer)
    base = lax.axis_index("own") * blocks
    ids_copy = pltpu.make_async_copy(ids_hbm, ids_ref, isem)
    owners_copy = pltpu.make_async_copy(owners_hbm, owners_ref, osem)
    x_copy = pltpu.make_async_copy(x_hbm, xbuf, xsem)
    m_copy = pltpu.make_async_copy(mom_hbm, mbuf.at[:, 0:peer], msem)
    ids_copy.start()
    owners_copy.start()
    x_copy.start()

    def b_copy(index, t):
        return pltpu.make_async_copy(b_hbm.at[index], bbuf.at[t], bsem.at[t])

    ids_copy.wait()
    first = ids_ref[base]
    last = ids_ref[base + blocks - 1]
    b_copy(first, 0).start()
    b_copy(jnp.minimum(first + 1, last), 1).start()
    m_copy.start()
    owners_copy.wait()

    for n in range(n_own):
        count_ref[n] = 0
    edge = blocks + 1
    meta_ref[blocks] = last - first + 1
    meta_ref[edge] = 0
    meta_ref[edge + 2] = blocks
    for k in range(blocks):
        meta_ref[edge + ids_ref[base + k] - first + 1] = k + 1
        owner = owners_ref[0, base + k]
        slot = count_ref[owner]
        count_ref[owner] = slot + 1
        owner_of[k] = owner
        rank_of[k] = slot
        pair = lax.shift_right_logical(slot, 1)
        source = jnp.where(pair < share, 0, 1)
        block = (source * n_own + owner) * share + pair - source * (pairs - share)
        meta_ref[k] = BR * block + lax.bitwise_and(slot, 1)
    meta_copy = pltpu.make_async_copy(meta_ref, meta_hbm, tsem)
    meta_copy.start()
    send_ref[:, 0 : BR * pairs, :] = jnp.zeros((n_own, BR * pairs, lanes), jnp.float32)
    if peer % 2:
        mbuf[:, peer] = jnp.zeros((n_own, BR, rank), jnp.float32)
    m_copy.wait()
    start = lax.axis_index("rep") * (pairs - share)
    for i in range(share):
        slot = 2 * (start + i)
        send_ref[:, BR * (pairs + i) : BR * (pairs + i + 1), :] = jnp.concatenate(
            [mbuf[:, slot], mbuf[:, slot + 1]], axis=2
        )
    x_copy.wait()
    rows = lax.broadcasted_iota(jnp.int32, fac.shape, 0)

    def pair_step(p, carry):
        m0 = first + 2 * p
        m1 = jnp.minimum(m0 + 1, last)

        @pl.when(p > 0)
        def _():
            b_copy(m0, 0).start()
            b_copy(m1, 1).start()

        b_copy(m0, 0).wait()
        b_copy(m1, 1).wait()
        first_basis = jnp.concatenate(split_parts(bbuf[0]), axis=0)
        second_basis = jnp.concatenate(split_parts(bbuf[1]), axis=0)
        split_ref[2 * p] = first_basis
        split_ref[2 * p + 1] = second_basis
        basis = jnp.concatenate([first_basis, second_basis], axis=0)
        high, low = split_parts(xbuf[...])
        total = 0.5 * (dot_nt(high, basis) + dot_nt(low, basis))
        both = []
        for part in (total[:, 0:lanes], total[:, lanes : 2 * lanes]):
            both.append(part + pltpu.roll(part, rank, 1))
        kept = jnp.where(rows < BR * meta_ref[edge + 2 * p + 1], both[0], both[1])
        fac[...] = jnp.where(rows < BR * meta_ref[edge + 2 * p], fac[...], kept)
        return carry

    lax.fori_loop(0, (last - first + 2) // 2, pair_step, 0)
    half = fac.shape[0] // 2
    f_ref[...] = jnp.where(
        upper_half(f_ref.shape), fac[half : 2 * half, :], fac[0:half, :]
    )
    upper = upper_half((BR, lanes)).astype(jnp.int32)
    for k in range(blocks):
        slot = rank_of[k]
        place = pl.ds(pl.multiple_of(lax.shift_right_logical(slot, 1) * BR, BR), BR)
        tile = send_ref[owner_of[k], place, :]
        mine = upper == lax.bitwise_and(slot, 1)
        send_ref[owner_of[k], place, :] = jnp.where(mine, fac[BR * k : BR * (k + 1), :], tile)
    meta_copy.wait()


def project_slabs(ids, owners, diff, bases_t, momentum):
    rows, width = diff.shape
    mats, rank, _ = bases_t.shape
    n_own, peer = momentum.shape[:2]
    pairs, share = send_plan(peer)
    blocks = rows // BR
    hbm = pl.BlockSpec(memory_space=pltpu.HBM)
    vmem = pl.BlockSpec(memory_space=pltpu.VMEM)
    return pl.pallas_call(
        project_kernel,
        out_shape=(
            jax.ShapeDtypeStruct((rows // 2, 2 * rank), jnp.float32),
            jax.ShapeDtypeStruct((n_own, BR * (pairs + share), 2 * rank), jnp.float32),
            jax.ShapeDtypeStruct((mats + mats % 2, 2 * rank, width), jnp.bfloat16),
            jax.ShapeDtypeStruct((meta_size(blocks, mats),), jnp.int32),
        ),
        in_specs=[hbm] * 5,
        out_specs=(vmem, vmem, vmem, hbm),
        scratch_shapes=[
            pltpu.SMEM(ids.shape, jnp.int32),
            pltpu.SMEM(owners.shape, jnp.int32),
            pltpu.SMEM((blocks,), jnp.int32),
            pltpu.SMEM((blocks,), jnp.int32),
            pltpu.SMEM((n_own,), jnp.int32),
            pltpu.SMEM((meta_size(blocks, mats),), jnp.int32),
            pltpu.VMEM((rows, width), jnp.float32),
            pltpu.VMEM((2, rank, width), jnp.float32),
            pltpu.VMEM((n_own, 2 * pairs, BR, rank), jnp.float32),
            pltpu.VMEM((rows, 2 * rank), jnp.float32),
            pltpu.SemaphoreType.DMA,
            pltpu.SemaphoreType.DMA,
            pltpu.SemaphoreType.DMA,
            pltpu.SemaphoreType.DMA((2,)),
            pltpu.SemaphoreType.DMA,
            pltpu.SemaphoreType.DMA,
        ],
        compiler_params=pltpu.CompilerParams(vmem_limit_bytes=VMEM_LIMIT),
        cost_estimate=pl.CostEstimate(
            flops=6 * rows * width * rank, bytes_accessed=6 << 20, transcendentals=0
        ),
        name="project_slabs",
    )(*[pltpu.with_memory_space_constraint(v, pltpu.HBM) for v in (ids, owners, diff, bases_t, momentum)])


def rebuild_kernel(
    meta_hbm, fmine_ref, fother_ref, mine_ref, other_ref, mom_ref, w_ref, split_ref,
    nm_hbm, out_hbm, meta_ref, obuf, nbuf, sent, lhs, gath, tsem, osem, nsem,
):
    lanes = gath.shape[1]
    rank = lanes // 2
    blocks = gath.shape[0] // BR
    n_own, peer = mom_ref.shape[:2]
    pairs, share = send_plan(peer)
    edge = blocks + 1
    rep = lax.axis_index("rep")
    meta_copy = pltpu.make_async_copy(meta_hbm, meta_ref, tsem)
    meta_copy.start()

    def o_copy(c):
        cols = pl.ds(COLUMNS[c], COLUMNS[c + 1] - COLUMNS[c])
        return pltpu.make_async_copy(obuf.at[:, cols], out_hbm.at[:, cols], osem.at[c])

    n_copy = pltpu.make_async_copy(nbuf, nm_hbm, nsem)
    span = n_own * BR * share
    for source, ref in ((rep, mine_ref), (1 - rep, other_ref)):
        place = pl.ds(pl.multiple_of(source * span, BR), span)
        sent[place, :] = ref[:, BR * pairs : BR * (pairs + share), :].reshape(span, lanes)
    arrived = mine_ref[:, 0 : BR * pairs, :] + other_ref[:, 0 : BR * pairs, :]
    for s in range(peer):
        block = arrived[:, BR * (s // 2) : BR * (s // 2 + 1), :]
        lane = rank * (s % 2)
        nbuf[:, s] = decay_rate * mom_ref[:, s] + block[:, :, lane : lane + rank]
    n_copy.start()
    average = fmine_ref[...] + fother_ref[...]
    turned = pltpu.roll(average, rank, 1)
    above = upper_half(average.shape)
    placed = jnp.concatenate(
        [jnp.where(above, turned, average), jnp.where(above, average, turned)], axis=0
    )
    upper = upper_half((BR, lanes)).astype(jnp.int32)
    meta_copy.wait()
    total = meta_ref[blocks]
    for k in range(blocks):
        odd = lax.bitwise_and(meta_ref[k], 1)
        tile = sent[pl.ds(pl.multiple_of(meta_ref[k] - odd, BR), BR), :]
        gath[BR * k : BR * (k + 1), :] = jnp.where(upper == odd, tile, 0.0)
    picked = gath[...]
    held = decay_rate * (picked + pltpu.roll(picked, rank, 1)) + placed
    step = -outer_rate * (placed + decay_rate * held)
    high = step.astype(jnp.bfloat16).astype(jnp.float32)
    parts = jnp.where(upper_half(step.shape), step - high, high)
    rows = lax.broadcasted_iota(jnp.int32, step.shape, 0)

    def left_rows(t):
        inside = (rows >= BR * meta_ref[edge + t]) & (rows < BR * meta_ref[edge + t + 1])
        return jnp.where(inside, parts, 0.0).astype(jnp.bfloat16)

    left0 = left_rows(0)
    left1 = left_rows(1)
    lhs[0] = left0
    lhs[1] = left1

    @pl.when(total > 2)
    def _():
        def fill(t, carry):
            lhs[t] = left_rows(t)
            return carry

        lax.fori_loop(2, total, fill, 0)

    def right_rows(t, c):
        start, stop = COLUMNS[c], COLUMNS[c + 1]
        top, bottom = split_ref[t, 0:rank, start:stop], split_ref[t, rank : 2 * rank, start:stop]
        return [top, top, bottom, bottom]

    def product(left, right):
        return jnp.dot(
            jnp.concatenate(left, axis=1),
            jnp.concatenate(right, axis=0),
            preferred_element_type=jnp.float32,
        )

    for c in range(len(COLUMNS) - 1):
        cols = slice(COLUMNS[c], COLUMNS[c + 1])

        @pl.when(total == 1)
        def _():
            one = product([lhs[0], lhs[0]], right_rows(0, c))
            obuf[:, cols] = w_ref[:, cols] + one

        @pl.when(total > 1)
        def _():
            two = product(
                [lhs[0], lhs[0], lhs[1], lhs[1]], right_rows(0, c) + right_rows(1, c)
            )
            obuf[:, cols] = w_ref[:, cols] + two

            def add_matrix(t, carry):
                obuf[:, cols] += product([lhs[t], lhs[t]], right_rows(t, c))
                return carry

            lax.fori_loop(2, total, add_matrix, 0)

        o_copy(c).start()
    for c in range(len(COLUMNS) - 1):
        o_copy(c).wait()
    n_copy.wait()


def rebuild_slabs(meta, fmine, fother, mine, other, momentum, weights, split):
    rows, width = weights.shape
    mats, lanes, _ = split.shape
    n_own, peer = momentum.shape[:2]
    _, share = send_plan(peer)
    vmem = pl.BlockSpec(memory_space=pltpu.VMEM)
    hbm = pl.BlockSpec(memory_space=pltpu.HBM)
    return pl.pallas_call(
        rebuild_kernel,
        out_shape=(
            jax.ShapeDtypeStruct(momentum.shape, jnp.float32),
            jax.ShapeDtypeStruct(weights.shape, jnp.float32),
        ),
        in_specs=[hbm] + [vmem] * 7,
        out_specs=(hbm, hbm),
        scratch_shapes=[
            pltpu.SMEM(meta.shape, jnp.int32),
            pltpu.VMEM((rows, width), jnp.float32),
            pltpu.VMEM(momentum.shape, jnp.float32),
            pltpu.VMEM((2 * n_own * BR * share, lanes), jnp.float32),
            pltpu.VMEM((mats, rows, lanes), jnp.bfloat16),
            pltpu.VMEM((rows, lanes), jnp.float32),
            pltpu.SemaphoreType.DMA,
            pltpu.SemaphoreType.DMA((len(COLUMNS) - 1,)),
            pltpu.SemaphoreType.DMA,
        ],
        compiler_params=pltpu.CompilerParams(vmem_limit_bytes=VMEM_LIMIT),
        cost_estimate=pl.CostEstimate(
            flops=8 * rows * width * lanes, bytes_accessed=8 << 20, transcendentals=0
        ),
        name="rebuild_slabs",
    )(meta, fmine, fother, mine, other, momentum, weights, split)


def per_device(weights, differences, bases, momentum, owners, matrix_ids):
    blocks, br, width = weights.shape
    swap = [(0, 1), (1, 0)]
    bases_t = jnp.swapaxes(bases, 1, 2)
    owner_row = owners.T
    fmine, packed, split, meta = project_slabs(
        matrix_ids, owner_row, differences.reshape(blocks * br, width), bases_t, momentum[0]
    )
    fother = lax.ppermute(fmine, "rep", swap)
    mine = lax.all_to_all(packed, "own", split_axis=0, concat_axis=0, tiled=True)
    other = lax.ppermute(mine, "rep", swap)
    new_momentum, new_weights = rebuild_slabs(
        meta, fmine, fother, mine, other, momentum[0],
        weights.reshape(blocks * br, width), split,
    )
    return (new_weights.reshape(weights.shape), new_momentum[None])


def solution(mesh):
    placed = (
        P("own", None, None),
        P("rep", "own", None, None),
        P(),
        P("own", None, None, None, None),
        P(),
        P(),
    )
    return jax.shard_map(
        per_device,
        mesh=mesh,
        in_specs=placed,
        out_specs=(P("own", None, None), P("own", None, None, None, None)),
        check_vma=False,
    )
```

time: 27.3 us -> 27 us (0.989)
  Pallas kernels: 8.15 us -> 7.85 us
    pallas_call x1, Pallas kernels: 3.4 us -> 3.08 us  [rebuild_slabs(): pl.pallas_call(rebuild_kernel, out_shape=(jax.ShapeDtypeStruct(momentum.s...]
where the time goes in v3:
time: 27 us; the launch traced here: 26.8 us
  blocking collectives  16.8 us (62%)
  Pallas kernels  7.85 us (29%)
  waiting for transfers between devices  1.03 us (4%)
  between operations  0.66 us (2%)
  starting transfers between devices  0.51 us (2%)
    all_to_all x1, blocking collectives, per_device(): lax.all_to_all(packed, 'own', split_axis=0, concat_axis=0, tiled=True)  16.8 us
    pallas_call x1, Pallas kernels, project_slabs(): pl.pallas_call(project_kernel, out_shape=(jax.ShapeDtypeStruct((rows // 2...  4.77 us
    pallas_call x1, Pallas kernels, rebuild_slabs(): pl.pallas_call(rebuild_kernel, out_shape=(jax.ShapeDtypeStruct(momentum.s...  3.08 us
    ppermute x1, waiting for transfers between devices, per_device(): fother = lax.ppermute(fmine, 'rep', swap)  1.02 us
  transfers between devices with their start and end apart: 2, of which 1 were waited for; matrix products, arithmetic and copies ran while one was open for 0% of the time, Pallas kernels for 0%

profile of v3, /device:TPU:0, one launch (start us, length us, event | category | flops | bytes accessed | tf_op | source)
XLA Modules:
  0.0 26.8 jit_solution(10267868172371982690)
XLA Ops:
  0.6 0.0 copy-start
  0.6 0.0 copy-start.1
  0.7 4.8 %project_slabs.1 = (f32[128,128]{1,0:T(8,128)S(1)}, f32[16,24,128]{2,1,0:T(8,128)S(1)}, bf16[6,128,4096]{2,1,0:T(8,128)(2,1)S(1)}, s32[128]{0:T(128)S(1)}) custom-call(s32[512]{0:T(512)} %ids_hbm.1, s32[1,512]{1,0:T(1,128)} %bitcast.12, f32[256,4096]{1,0:T(8,128)} %bitcast.11, f32[6,64,4096]{2,1,0:T(8,128)} %bitcast.10, f32[16,4,8,64]{3,2,1,0:T(8,128)} %bitcast.8), custom_call_target="tpu_custom_call" | custom-call | flops 402653184 | bytes 6291456 | tf_op jit(solution)/shard_map/project_slabs/pallas_call | solution.py:148
  5.4 16.8 %all_to_all.5.mine_ref = f32[16,24,128]{2,1,0:T(8,128)S(1)} all-to-all(f32[16,24,128]{2,1,0:T(8,128)S(1)} %get-tuple-element.10), channel_id=1, replica_groups=mesh['rep'=2,'own'=16] {'own'}, dimensions={0} | all-to-all | bytes 393216 | tf_op jit(solution)/shard_map/all_to_all | solution.py:332
  22.2 0.0 collective-permute-start.1
  22.2 0.5 %collective-permute-start = (f32[128,128]{1,0:T(8,128)S(1)}, f32[128,128]{1,0:T(8,128)S(1)}, u32[]{:S(2)}, u32[]{:S(2)}) collective-permute-start(f32[128,128]{1,0:T(8,128)S(1)} %get-tuple-element.9.fmine_ref), channel_id=1, source_target_pairs={{0,16},{16,0},{1,17},{17,1},{2,18},{18,2},{3,19},{19,3},{4,20},{20... | collective-permute-start | bytes 196616 | tf_op jit(solution)/shard_map/ppermute | solution.py:331
  22.7 1.0 %collective-permute-done.fother_ref = f32[128,128]{1,0:T(8,128)S(1)} collective-permute-done((f32[128,128]{1,0:T(8,128)S(1)}, f32[128,128]{1,0:T(8,128)S(1)}, u32[]{:S(2)}, u32[]{:S(2)}) %collective-permute-start) | collective-permute-done | bytes 65568 | tf_op jit(solution)/shard_map/ppermute | solution.py:331
  23.7 0.0 collective-permute-done.1.other_ref
  23.7 0.0 copy-done
  23.7 0.0 copy-done.1
  23.7 3.1 %rebuild_slabs.1 = (f32[16,4,8,64]{3,2,1,0:T(8,128)}, f32[256,4096]{1,0:T(8,128)}) custom-call(s32[128]{0:T(128)S(1)} %get-tuple-element.8.meta_hbm, f32[128,128]{1,0:T(8,128)S(1)} %get-tuple-element.9.fmine_ref, f32[128,128]{1,0:T(8,128)S(1)} %collective-permute-done.fother_ref, f32[16,24,128]{2,1,0:T(8,128)S(1)} %all_to_all.5.mine_ref, ...), custom_call_target="tpu_custom_call" | custom-call | flops 1073741824 | bytes 8388608 | tf_op jit(solution)/shard_map/rebuild_slabs/pallas_call | solution.py:296
Async XLA Ops:
  0.6 23.1 %copy-start = (f32[32,8,4096]{2,1,0:T(8,128)S(1)}, f32[32,8,4096]{2,1,0:T(8,128)}, u32[]{:S(2)}) copy-start(f32[32,8,4096]{2,1,0:T(8,128)} %param.6) | copy-start | bytes 12582916
  0.6 23.1 %copy-start.1 = (f32[1,16,4,8,64]{4,3,2,1,0:T(8,128)S(1)}, f32[1,16,4,8,64]{4,3,2,1,0:T(8,128)}, u32[]{:S(2)}) copy-start(f32[1,16,4,8,64]{4,3,2,1,0:T(8,128)} %param.9) | copy-start | bytes 393220
  22.2 1.5 %collective-permute-start.1 = (f32[16,24,128]{2,1,0:T(8,128)S(1)}, f32[16,24,128]{2,1,0:T(8,128)S(1)}, u32[]{:S(2)}, u32[]{:S(2)}) collective-permute-start(f32[16,24,128]{2,1,0:T(8,128)S(1)} %all_to_all.5.mine_ref), channel_id=1, source_target_pairs={{0,16},{16,0},{1,17},{17,1},{2,18},{18,2},{3,19},{19,3},{4,20},{20... | collective-permute-start | bytes 589832 | tf_op jit(solution)/shard_map/ppermute | solution.py:333
  22.2 1.5 %collective-permute-start = (f32[128,128]{1,0:T(8,128)S(1)}, f32[128,128]{1,0:T(8,128)S(1)}, u32[]{:S(2)}, u32[]{:S(2)}) collective-permute-start(f32[128,128]{1,0:T(8,128)S(1)} %get-tuple-element.9.fmine_ref), channel_id=1, source_target_pairs={{0,16},{16,0},{1,17},{17,1},{2,18},{18,2},{3,19},{19,3},{4,20},{20... | collective-permute-start | bytes 196616 | tf_op jit(solution)/shard_map/ppermute | solution.py:331

commit v4 on v3

--- a/solution.py
+++ b/solution.py
@@ -32,13 +32,13 @@
 
 
 def meta_size(blocks, mats):
-    return -(-(blocks + mats + 4) // 128) * 128
+    return -(-(blocks + mats + 4) // 8) * 8
 
 
 def project_kernel(
-    ids_hbm, owners_hbm, x_hbm, b_hbm, mom_hbm, f_ref, send_ref, split_ref, meta_hbm,
+    ids_hbm, owners_hbm, x_hbm, b_hbm, mom_hbm, f_ref, send_ref, split_ref, table_ref,
     ids_ref, owners_ref, owner_of, rank_of, count_ref, meta_ref,
-    xbuf, bbuf, mbuf, fac, isem, osem, xsem, bsem, msem, tsem,
+    xbuf, bbuf, mbuf, fac, isem, osem, xsem, bsem, msem,
 ):
     blocks = x_hbm.shape[0] // BR
     lanes = send_ref.shape[2]
@@ -70,7 +70,8 @@
     edge = blocks + 1
     meta_ref[blocks] = last - first + 1
     meta_ref[edge] = 0
-    meta_ref[edge + 2] = blocks
+    for n in range(edge + 1, table_ref.shape[0]):
+        meta_ref[n] = blocks
     for k in range(blocks):
         meta_ref[edge + ids_ref[base + k] - first + 1] = k + 1
         owner = owners_ref[0, base + k]
@@ -82,8 +83,8 @@
         source = jnp.where(pair < share, 0, 1)
         block = (source * n_own + owner) * share + pair - source * (pairs - share)
         meta_ref[k] = BR * block + lax.bitwise_and(slot, 1)
-    meta_copy = pltpu.make_async_copy(meta_ref, meta_hbm, tsem)
-    meta_copy.start()
+    for n in range(table_ref.shape[0]):
+        table_ref[n : n + 1, :] = jnp.full((1, lanes), meta_ref[n], jnp.int32)
     send_ref[:, 0 : BR * pairs, :] = jnp.zeros((n_own, BR * pairs, lanes), jnp.float32)
     if peer % 2:
         mbuf[:, peer] = jnp.zeros((n_own, BR, rank), jnp.float32)
@@ -134,7 +135,6 @@
         tile = send_ref[owner_of[k], place, :]
         mine = upper == lax.bitwise_and(slot, 1)
         send_ref[owner_of[k], place, :] = jnp.where(mine, fac[BR * k : BR * (k + 1), :], tile)
-    meta_copy.wait()
 
 
 def project_slabs(ids, owners, diff, bases_t, momentum):
@@ -151,10 +151,10 @@
             jax.ShapeDtypeStruct((rows // 2, 2 * rank), jnp.float32),
             jax.ShapeDtypeStruct((n_own, BR * (pairs + share), 2 * rank), jnp.float32),
             jax.ShapeDtypeStruct((mats + mats % 2, 2 * rank, width), jnp.bfloat16),
-            jax.ShapeDtypeStruct((meta_size(blocks, mats),), jnp.int32),
+            jax.ShapeDtypeStruct((meta_size(blocks, mats), 2 * rank), jnp.int32),
         ),
         in_specs=[hbm] * 5,
-        out_specs=(vmem, vmem, vmem, hbm),
+        out_specs=(vmem,) * 4,
         scratch_shapes=[
             pltpu.SMEM(ids.shape, jnp.int32),
             pltpu.SMEM(owners.shape, jnp.int32),
@@ -171,7 +171,6 @@
             pltpu.SemaphoreType.DMA,
             pltpu.SemaphoreType.DMA((2,)),
             pltpu.SemaphoreType.DMA,
-            pltpu.SemaphoreType.DMA,
         ],
         compiler_params=pltpu.CompilerParams(vmem_limit_bytes=VMEM_LIMIT),
         cost_estimate=pl.CostEstimate(
@@ -182,8 +181,8 @@
 
 
 def rebuild_kernel(
-    meta_hbm, fmine_ref, fother_ref, mine_ref, other_ref, mom_ref, w_ref, split_ref,
-    nm_hbm, out_hbm, meta_ref, obuf, nbuf, sent, lhs, gath, tsem, osem, nsem,
+    table_ref, fmine_ref, fother_ref, mine_ref, other_ref, mom_ref, w_ref, split_ref,
+    nm_hbm, out_hbm, obuf, nbuf, sent, lhs, gath, osem, nsem,
 ):
     lanes = gath.shape[1]
     rank = lanes // 2
@@ -192,8 +191,6 @@
     pairs, share = send_plan(peer)
     edge = blocks + 1
     rep = lax.axis_index("rep")
-    meta_copy = pltpu.make_async_copy(meta_hbm, meta_ref, tsem)
-    meta_copy.start()
 
     def o_copy(c):
         cols = pl.ds(COLUMNS[c], COLUMNS[c + 1] - COLUMNS[c])
@@ -217,11 +214,11 @@
         [jnp.where(above, turned, average), jnp.where(above, average, turned)], axis=0
     )
     upper = upper_half((BR, lanes)).astype(jnp.int32)
-    meta_copy.wait()
-    total = meta_ref[blocks]
+    total = table_ref[blocks : blocks + 1, 0:1][0, 0]
     for k in range(blocks):
-        odd = lax.bitwise_and(meta_ref[k], 1)
-        tile = sent[pl.ds(pl.multiple_of(meta_ref[k] - odd, BR), BR), :]
+        odd = lax.bitwise_and(table_ref[k : k + 1, :], 1)
+        row = lax.bitwise_and(table_ref[k : k + 1, 0:1][0, 0], -BR)
+        tile = sent[pl.ds(pl.multiple_of(row, BR), BR), :]
         gath[BR * k : BR * (k + 1), :] = jnp.where(upper == odd, tile, 0.0)
     picked = gath[...]
     held = decay_rate * (picked + pltpu.roll(picked, rank, 1)) + placed
@@ -231,7 +228,9 @@
     rows = lax.broadcasted_iota(jnp.int32, step.shape, 0)
 
     def left_rows(t):
-        inside = (rows >= BR * meta_ref[edge + t]) & (rows < BR * meta_ref[edge + t + 1])
+        start = BR * table_ref[pl.ds(edge + t, 1), :]
+        stop = BR * table_ref[pl.ds(edge + t + 1, 1), :]
+        inside = (rows >= start) & (rows < stop)
         return jnp.where(inside, parts, 0.0).astype(jnp.bfloat16)
 
     left0 = left_rows(0)
@@ -299,16 +298,14 @@
             jax.ShapeDtypeStruct(momentum.shape, jnp.float32),
             jax.ShapeDtypeStruct(weights.shape, jnp.float32),
         ),
-        in_specs=[hbm] + [vmem] * 7,
+        in_specs=[vmem] * 8,
         out_specs=(hbm, hbm),
         scratch_shapes=[
-            pltpu.SMEM(meta.shape, jnp.int32),
             pltpu.VMEM((rows, width), jnp.float32),
             pltpu.VMEM(momentum.shape, jnp.float32),
             pltpu.VMEM((2 * n_own * BR * share, lanes), jnp.float32),
             pltpu.VMEM((mats, rows, lanes), jnp.bfloat16),
             pltpu.VMEM((rows, lanes), jnp.float32),
-            pltpu.SemaphoreType.DMA,
             pltpu.SemaphoreType.DMA((len(COLUMNS) - 1,)),
             pltpu.SemaphoreType.DMA,
         ],

time: 27 us -> 26.5 us (0.981)
  Pallas kernels: 7.85 us -> 7.35 us
    pallas_call x1, Pallas kernels: 3.08 us -> 2.6 us  [rebuild_slabs(): pl.pallas_call(rebuild_kernel, out_shape=(jax.ShapeDtypeStruct(momentum.s...]
where the time goes in v4:
time: 26.5 us; the launch traced here: 26.3 us
  blocking collectives  16.8 us (63%)
  Pallas kernels  7.35 us (28%)
  waiting for transfers between devices  1.03 us (4%)
  between operations  0.66 us (2%)
  starting transfers between devices  0.51 us (2%)
    all_to_all x1, blocking collectives, per_device(): lax.all_to_all(packed, 'own', split_axis=0, concat_axis=0, tiled=True)  16.8 us
    pallas_call x1, Pallas kernels, project_slabs(): pl.pallas_call(project_kernel, out_shape=(jax.ShapeDtypeStruct((rows // 2...  4.75 us
    pallas_call x1, Pallas kernels, rebuild_slabs(): pl.pallas_call(rebuild_kernel, out_shape=(jax.ShapeDtypeStruct(momentum.s...  2.6 us
    ppermute x1, waiting for transfers between devices, per_device(): fother = lax.ppermute(fmine, 'rep', swap)  1.02 us
  transfers between devices with their start and end apart: 2, of which 1 were waited for; matrix products, arithmetic and copies ran while one was open for 0% of the time, Pallas kernels for 0%

profile of v4, /device:TPU:0, one launch (start us, length us, event | category | flops | bytes accessed | tf_op | source)
XLA Modules:
  0.0 26.3 jit_solution(4642214024282611405)
XLA Ops:
  0.6 0.0 copy-start
  0.6 0.0 copy-start.1
  0.7 4.7 %project_slabs.1 = (f32[128,128]{1,0:T(8,128)S(1)}, f32[16,24,128]{2,1,0:T(8,128)S(1)}, bf16[6,128,4096]{2,1,0:T(8,128)(2,1)S(1)}, s32[48,128]{1,0:T(8,128)S(1)}) custom-call(s32[512]{0:T(512)} %ids_hbm.1, s32[1,512]{1,0:T(1,128)} %bitcast.12, f32[256,4096]{1,0:T(8,128)} %bitcast.11, f32[6,64,4096]{2,1,0:T(8,128)} %bitcast.10, f32[16,4,8,64]{3,2,1,0:T(8,128)} %bitcast.8), custom_call_target="tpu_custom_call" | custom-call | flops 402653184 | bytes 6291456 | tf_op jit(solution)/shard_map/project_slabs/pallas_call | solution.py:148
  5.4 16.8 %all_to_all.5.mine_ref = f32[16,24,128]{2,1,0:T(8,128)S(1)} all-to-all(f32[16,24,128]{2,1,0:T(8,128)S(1)} %get-tuple-element.10), channel_id=1, replica_groups=mesh['rep'=2,'own'=16] {'own'}, dimensions={0} | all-to-all | bytes 393216 | tf_op jit(solution)/shard_map/all_to_all | solution.py:329
  22.2 0.0 collective-permute-start.1
  22.2 0.5 %collective-permute-start = (f32[128,128]{1,0:T(8,128)S(1)}, f32[128,128]{1,0:T(8,128)S(1)}, u32[]{:S(2)}, u32[]{:S(2)}) collective-permute-start(f32[128,128]{1,0:T(8,128)S(1)} %get-tuple-element.9.fmine_ref), channel_id=1, source_target_pairs={{0,16},{16,0},{1,17},{17,1},{2,18},{18,2},{3,19},{19,3},{4,20},{20... | collective-permute-start | bytes 196616 | tf_op jit(solution)/shard_map/ppermute | solution.py:328
  22.7 1.0 %collective-permute-done.fother_ref = f32[128,128]{1,0:T(8,128)S(1)} collective-permute-done((f32[128,128]{1,0:T(8,128)S(1)}, f32[128,128]{1,0:T(8,128)S(1)}, u32[]{:S(2)}, u32[]{:S(2)}) %collective-permute-start) | collective-permute-done | bytes 65568 | tf_op jit(solution)/shard_map/ppermute | solution.py:328
  23.7 0.0 collective-permute-done.1.other_ref
  23.7 0.0 copy-done
  23.7 0.0 copy-done.1
  23.7 2.6 %rebuild_slabs.1 = (f32[16,4,8,64]{3,2,1,0:T(8,128)}, f32[256,4096]{1,0:T(8,128)}) custom-call(s32[48,128]{1,0:T(8,128)S(1)} %get-tuple-element.8.table_ref, f32[128,128]{1,0:T(8,128)S(1)} %get-tuple-element.9.fmine_ref, f32[128,128]{1,0:T(8,128)S(1)} %collective-permute-done.fother_ref, f32[16,24,128]{2,1,0:T(8,128)S(1)} %all_to_all.5.mine_ref, ...), custom_call_target="tpu_custom_call" | custom-call | flops 1073741824 | bytes 8388608 | tf_op jit(solution)/shard_map/rebuild_slabs/pallas_call | solution.py:295
Async XLA Ops:
  0.6 23.1 %copy-start = (f32[32,8,4096]{2,1,0:T(8,128)S(1)}, f32[32,8,4096]{2,1,0:T(8,128)}, u32[]{:S(2)}) copy-start(f32[32,8,4096]{2,1,0:T(8,128)} %param.6) | copy-start | bytes 12582916
  0.6 23.1 %copy-start.1 = (f32[1,16,4,8,64]{4,3,2,1,0:T(8,128)S(1)}, f32[1,16,4,8,64]{4,3,2,1,0:T(8,128)}, u32[]{:S(2)}) copy-start(f32[1,16,4,8,64]{4,3,2,1,0:T(8,128)} %param.9) | copy-start | bytes 393220
  22.2 1.5 %collective-permute-start.1 = (f32[16,24,128]{2,1,0:T(8,128)S(1)}, f32[16,24,128]{2,1,0:T(8,128)S(1)}, u32[]{:S(2)}, u32[]{:S(2)}) collective-permute-start(f32[16,24,128]{2,1,0:T(8,128)S(1)} %all_to_all.5.mine_ref), channel_id=1, source_target_pairs={{0,16},{16,0},{1,17},{17,1},{2,18},{18,2},{3,19},{19,3},{4,20},{20... | collective-permute-start | bytes 589832 | tf_op jit(solution)/shard_map/ppermute | solution.py:330
  22.2 1.5 %collective-permute-start = (f32[128,128]{1,0:T(8,128)S(1)}, f32[128,128]{1,0:T(8,128)S(1)}, u32[]{:S(2)}, u32[]{:S(2)}) collective-permute-start(f32[128,128]{1,0:T(8,128)S(1)} %get-tuple-element.9.fmine_ref), channel_id=1, source_target_pairs={{0,16},{16,0},{1,17},{17,1},{2,18},{18,2},{3,19},{19,3},{4,20},{20... | collective-permute-start | bytes 196616 | tf_op jit(solution)/shard_map/ppermute | solution.py:328

commit v5 on v4

--- a/solution.py
+++ b/solution.py
@@ -61,7 +61,11 @@
     first = ids_ref[base]
     last = ids_ref[base + blocks - 1]
     b_copy(first, 0).start()
-    b_copy(jnp.minimum(first + 1, last), 1).start()
+
+    @pl.when(first < last)
+    def _():
+        b_copy(first + 1, 1).start()
+
     m_copy.start()
     owners_copy.wait()
 
@@ -100,17 +104,24 @@
 
     def pair_step(p, carry):
         m0 = first + 2 * p
-        m1 = jnp.minimum(m0 + 1, last)
+        paired = m0 < last
 
         @pl.when(p > 0)
         def _():
             b_copy(m0, 0).start()
-            b_copy(m1, 1).start()
+
+        @pl.when((p > 0) & paired)
+        def _():
+            b_copy(m0 + 1, 1).start()
 
         b_copy(m0, 0).wait()
-        b_copy(m1, 1).wait()
+
+        @pl.when(paired)
+        def _():
+            b_copy(m0 + 1, 1).wait()
+
         first_basis = jnp.concatenate(split_parts(bbuf[0]), axis=0)
-        second_basis = jnp.concatenate(split_parts(bbuf[1]), axis=0)
+        second_basis = jnp.concatenate(split_parts(bbuf[jnp.where(paired, 1, 0)]), axis=0)
         split_ref[2 * p] = first_basis
         split_ref[2 * p + 1] = second_basis
         basis = jnp.concatenate([first_basis, second_basis], axis=0)

time: 26.5 us -> 26.4 us (level); the launches traced: 26.3 us -> 26.5 us
  Pallas kernels: 7.35 us -> 7.79 us
  blocking collectives: 16.8 us -> 16.5 us
    pallas_call x1, Pallas kernels: 2.6 us -> 3.04 us  [rebuild_slabs(): pl.pallas_call(rebuild_kernel, out_shape=(jax.ShapeDtypeStruct(momentum.s...]
    all_to_all x1, blocking collectives: 16.8 us -> 16.5 us  [per_device(): lax.all_to_all(packed, 'own', split_axis=0, concat_axis=0, tiled=True)]
where the time goes in v5:
time: 26.4 us; the launch traced here: 26.5 us
  blocking collectives  16.5 us (62%)
  Pallas kernels  7.79 us (30%)
  waiting for transfers between devices  1.03 us (4%)
  between operations  0.66 us (2%)
  starting transfers between devices  0.51 us (2%)
    all_to_all x1, blocking collectives, per_device(): lax.all_to_all(packed, 'own', split_axis=0, concat_axis=0, tiled=True)  16.5 us
    pallas_call x1, Pallas kernels, project_slabs(): pl.pallas_call(project_kernel, out_shape=(jax.ShapeDtypeStruct((rows // 2...  4.75 us
    pallas_call x1, Pallas kernels, rebuild_slabs(): pl.pallas_call(rebuild_kernel, out_shape=(jax.ShapeDtypeStruct(momentum.s...  3.04 us
    ppermute x1, waiting for transfers between devices, per_device(): fother = lax.ppermute(fmine, 'rep', swap)  1.02 us
  transfers between devices with their start and end apart: 2, of which 1 were waited for; matrix products, arithmetic and copies ran while one was open for 0% of the time, Pallas kernels for 0%

profile of v5, /device:TPU:0, one launch (start us, length us, event | category | flops | bytes accessed | tf_op | source)
XLA Modules:
  0.0 26.5 jit_solution(5725424563034522809)
XLA Ops:
  0.6 0.0 copy-start
  0.6 0.0 copy-start.1
  0.7 4.8 %project_slabs.1 = (f32[128,128]{1,0:T(8,128)S(1)}, f32[16,24,128]{2,1,0:T(8,128)S(1)}, bf16[6,128,4096]{2,1,0:T(8,128)(2,1)S(1)}, s32[48,128]{1,0:T(8,128)S(1)}) custom-call(s32[512]{0:T(512)} %ids_hbm.1, s32[1,512]{1,0:T(1,128)} %bitcast.12, f32[256,4096]{1,0:T(8,128)} %bitcast.11, f32[6,64,4096]{2,1,0:T(8,128)} %bitcast.10, f32[16,4,8,64]{3,2,1,0:T(8,128)} %bitcast.8), custom_call_target="tpu_custom_call" | custom-call | flops 402653184 | bytes 6291456 | tf_op jit(solution)/shard_map/project_slabs/pallas_call | solution.py:159
  5.4 16.5 %all_to_all.5.mine_ref = f32[16,24,128]{2,1,0:T(8,128)S(1)} all-to-all(f32[16,24,128]{2,1,0:T(8,128)S(1)} %get-tuple-element.10), channel_id=1, replica_groups=mesh['rep'=2,'own'=16] {'own'}, dimensions={0} | all-to-all | bytes 393216 | tf_op jit(solution)/shard_map/all_to_all | solution.py:340
  21.9 0.0 collective-permute-start.1
  21.9 0.5 %collective-permute-start = (f32[128,128]{1,0:T(8,128)S(1)}, f32[128,128]{1,0:T(8,128)S(1)}, u32[]{:S(2)}, u32[]{:S(2)}) collective-permute-start(f32[128,128]{1,0:T(8,128)S(1)} %get-tuple-element.9.fmine_ref), channel_id=1, source_target_pairs={{0,16},{16,0},{1,17},{17,1},{2,18},{18,2},{3,19},{19,3},{4,20},{20... | collective-permute-start | bytes 196616 | tf_op jit(solution)/shard_map/ppermute | solution.py:339
  22.4 1.0 %collective-permute-done.fother_ref = f32[128,128]{1,0:T(8,128)S(1)} collective-permute-done((f32[128,128]{1,0:T(8,128)S(1)}, f32[128,128]{1,0:T(8,128)S(1)}, u32[]{:S(2)}, u32[]{:S(2)}) %collective-permute-start) | collective-permute-done | bytes 65568 | tf_op jit(solution)/shard_map/ppermute | solution.py:339
  23.4 0.0 collective-permute-done.1.other_ref
  23.4 0.0 copy-done
  23.4 0.0 copy-done.1
  23.4 3.0 %rebuild_slabs.1 = (f32[16,4,8,64]{3,2,1,0:T(8,128)}, f32[256,4096]{1,0:T(8,128)}) custom-call(s32[48,128]{1,0:T(8,128)S(1)} %get-tuple-element.8.table_ref, f32[128,128]{1,0:T(8,128)S(1)} %get-tuple-element.9.fmine_ref, f32[128,128]{1,0:T(8,128)S(1)} %collective-permute-done.fother_ref, f32[16,24,128]{2,1,0:T(8,128)S(1)} %all_to_all.5.mine_ref, ...), custom_call_target="tpu_custom_call" | custom-call | flops 1073741824 | bytes 8388608 | tf_op jit(solution)/shard_map/rebuild_slabs/pallas_call | solution.py:306
Async XLA Ops:
  0.6 22.8 %copy-start = (f32[32,8,4096]{2,1,0:T(8,128)S(1)}, f32[32,8,4096]{2,1,0:T(8,128)}, u32[]{:S(2)}) copy-start(f32[32,8,4096]{2,1,0:T(8,128)} %param.6) | copy-start | bytes 12582916
  0.6 22.8 %copy-start.1 = (f32[1,16,4,8,64]{4,3,2,1,0:T(8,128)S(1)}, f32[1,16,4,8,64]{4,3,2,1,0:T(8,128)}, u32[]{:S(2)}) copy-start(f32[1,16,4,8,64]{4,3,2,1,0:T(8,128)} %param.9) | copy-start | bytes 393220
  21.9 1.5 %collective-permute-start.1 = (f32[16,24,128]{2,1,0:T(8,128)S(1)}, f32[16,24,128]{2,1,0:T(8,128)S(1)}, u32[]{:S(2)}, u32[]{:S(2)}) collective-permute-start(f32[16,24,128]{2,1,0:T(8,128)S(1)} %all_to_all.5.mine_ref), channel_id=1, source_target_pairs={{0,16},{16,0},{1,17},{17,1},{2,18},{18,2},{3,19},{19,3},{4,20},{20... | collective-permute-start | bytes 589832 | tf_op jit(solution)/shard_map/ppermute | solution.py:341
  21.9 1.5 %collective-permute-start = (f32[128,128]{1,0:T(8,128)S(1)}, f32[128,128]{1,0:T(8,128)S(1)}, u32[]{:S(2)}, u32[]{:S(2)}) collective-permute-start(f32[128,128]{1,0:T(8,128)S(1)} %get-tuple-element.9.fmine_ref), channel_id=1, source_target_pairs={{0,16},{16,0},{1,17},{17,1},{2,18},{18,2},{3,19},{19,3},{4,20},{20... | collective-permute-start | bytes 196616 | tf_op jit(solution)/shard_map/ppermute | solution.py:339

commit v6 on v5

--- a/solution.py
+++ b/solution.py
@@ -143,9 +143,8 @@
     for k in range(blocks):
         slot = rank_of[k]
         place = pl.ds(pl.multiple_of(lax.shift_right_logical(slot, 1) * BR, BR), BR)
-        tile = send_ref[owner_of[k], place, :]
         mine = upper == lax.bitwise_and(slot, 1)
-        send_ref[owner_of[k], place, :] = jnp.where(mine, fac[BR * k : BR * (k + 1), :], tile)
+        pltpu.store(send_ref.at[owner_of[k], place, :], fac[BR * k : BR * (k + 1), :], mask=mine)
 
 
 def project_slabs(ids, owners, diff, bases_t, momentum):

time: 26.4 us -> 26.2 us (level); the launches traced: 26.5 us -> 26 us
  Pallas kernels: 7.79 us -> 7.02 us
  blocking collectives: 16.5 us -> 16.8 us
    pallas_call x1, Pallas kernels: 3.04 us -> 2.6 us  [rebuild_slabs(): pl.pallas_call(rebuild_kernel, out_shape=(jax.ShapeDtypeStruct(momentum.s...]
    pallas_call x1, Pallas kernels: 4.75 us -> 4.42 us  [project_slabs(): pl.pallas_call(project_kernel, out_shape=(jax.ShapeDtypeStruct((rows // 2...]
where the time goes in v6:
time: 26.2 us; the launch traced here: 26 us
  blocking collectives  16.8 us (64%)
  Pallas kernels  7.02 us (27%)
  waiting for transfers between devices  1.03 us (4%)
  between operations  0.66 us (3%)
  starting transfers between devices  0.51 us (2%)
    all_to_all x1, blocking collectives, per_device(): lax.all_to_all(packed, 'own', split_axis=0, concat_axis=0, tiled=True)  16.8 us
    pallas_call x1, Pallas kernels, project_slabs(): pl.pallas_call(project_kernel, out_shape=(jax.ShapeDtypeStruct((rows // 2...  4.42 us
    pallas_call x1, Pallas kernels, rebuild_slabs(): pl.pallas_call(rebuild_kernel, out_shape=(jax.ShapeDtypeStruct(momentum.s...  2.6 us
    ppermute x1, waiting for transfers between devices, per_device(): fother = lax.ppermute(fmine, 'rep', swap)  1.02 us
  transfers between devices with their start and end apart: 2, of which 1 were waited for; matrix products, arithmetic and copies ran while one was open for 0% of the time, Pallas kernels for 0%

profile of v6, /device:TPU:0, one launch (start us, length us, event | category | flops | bytes accessed | tf_op | source)
XLA Modules:
  0.0 26.0 jit_solution(2581233051234715725)
XLA Ops:
  0.6 0.0 copy-start
  0.6 0.0 copy-start.1
  0.7 4.4 %project_slabs.1 = (f32[128,128]{1,0:T(8,128)S(1)}, f32[16,24,128]{2,1,0:T(8,128)S(1)}, bf16[6,128,4096]{2,1,0:T(8,128)(2,1)S(1)}, s32[48,128]{1,0:T(8,128)S(1)}) custom-call(s32[512]{0:T(512)} %ids_hbm.1, s32[1,512]{1,0:T(1,128)} %bitcast.12, f32[256,4096]{1,0:T(8,128)} %bitcast.11, f32[6,64,4096]{2,1,0:T(8,128)} %bitcast.10, f32[16,4,8,64]{3,2,1,0:T(8,128)} %bitcast.8), custom_call_target="tpu_custom_call" | custom-call | flops 402653184 | bytes 6291456 | tf_op jit(solution)/shard_map/project_slabs/pallas_call | solution.py:158
  5.1 16.8 %all_to_all.5.mine_ref = f32[16,24,128]{2,1,0:T(8,128)S(1)} all-to-all(f32[16,24,128]{2,1,0:T(8,128)S(1)} %get-tuple-element.10), channel_id=1, replica_groups=mesh['rep'=2,'own'=16] {'own'}, dimensions={0} | all-to-all | bytes 393216 | tf_op jit(solution)/shard_map/all_to_all | solution.py:339
  21.8 0.0 collective-permute-start.1
  21.8 0.5 %collective-permute-start = (f32[128,128]{1,0:T(8,128)S(1)}, f32[128,128]{1,0:T(8,128)S(1)}, u32[]{:S(2)}, u32[]{:S(2)}) collective-permute-start(f32[128,128]{1,0:T(8,128)S(1)} %get-tuple-element.9.fmine_ref), channel_id=1, source_target_pairs={{0,16},{16,0},{1,17},{17,1},{2,18},{18,2},{3,19},{19,3},{4,20},{20... | collective-permute-start | bytes 196616 | tf_op jit(solution)/shard_map/ppermute | solution.py:338
  22.3 1.0 %collective-permute-done.fother_ref = f32[128,128]{1,0:T(8,128)S(1)} collective-permute-done((f32[128,128]{1,0:T(8,128)S(1)}, f32[128,128]{1,0:T(8,128)S(1)}, u32[]{:S(2)}, u32[]{:S(2)}) %collective-permute-start) | collective-permute-done | bytes 65568 | tf_op jit(solution)/shard_map/ppermute | solution.py:338
  23.4 0.0 collective-permute-done.1.other_ref
  23.4 0.0 copy-done
  23.4 0.0 copy-done.1
  23.4 2.6 %rebuild_slabs.1 = (f32[16,4,8,64]{3,2,1,0:T(8,128)}, f32[256,4096]{1,0:T(8,128)}) custom-call(s32[48,128]{1,0:T(8,128)S(1)} %get-tuple-element.8.table_ref, f32[128,128]{1,0:T(8,128)S(1)} %get-tuple-element.9.fmine_ref, f32[128,128]{1,0:T(8,128)S(1)} %collective-permute-done.fother_ref, f32[16,24,128]{2,1,0:T(8,128)S(1)} %all_to_all.5.mine_ref, ...), custom_call_target="tpu_custom_call" | custom-call | flops 1073741824 | bytes 8388608 | tf_op jit(solution)/shard_map/rebuild_slabs/pallas_call | solution.py:305
Async XLA Ops:
  0.6 22.7 %copy-start = (f32[32,8,4096]{2,1,0:T(8,128)S(1)}, f32[32,8,4096]{2,1,0:T(8,128)}, u32[]{:S(2)}) copy-start(f32[32,8,4096]{2,1,0:T(8,128)} %param.6) | copy-start | bytes 12582916
  0.6 22.7 %copy-start.1 = (f32[1,16,4,8,64]{4,3,2,1,0:T(8,128)S(1)}, f32[1,16,4,8,64]{4,3,2,1,0:T(8,128)}, u32[]{:S(2)}) copy-start(f32[1,16,4,8,64]{4,3,2,1,0:T(8,128)} %param.9) | copy-start | bytes 393220
  21.8 1.5 %collective-permute-start.1 = (f32[16,24,128]{2,1,0:T(8,128)S(1)}, f32[16,24,128]{2,1,0:T(8,128)S(1)}, u32[]{:S(2)}, u32[]{:S(2)}) collective-permute-start(f32[16,24,128]{2,1,0:T(8,128)S(1)} %all_to_all.5.mine_ref), channel_id=1, source_target_pairs={{0,16},{16,0},{1,17},{17,1},{2,18},{18,2},{3,19},{19,3},{4,20},{20... | collective-permute-start | bytes 589832 | tf_op jit(solution)/shard_map/ppermute | solution.py:340
  21.8 1.5 %collective-permute-start = (f32[128,128]{1,0:T(8,128)S(1)}, f32[128,128]{1,0:T(8,128)S(1)}, u32[]{:S(2)}, u32[]{:S(2)}) collective-permute-start(f32[128,128]{1,0:T(8,128)S(1)} %get-tuple-element.9.fmine_ref), channel_id=1, source_target_pairs={{0,16},{16,0},{1,17},{17,1},{2,18},{18,2},{3,19},{19,3},{4,20},{20... | collective-permute-start | bytes 196616 | tf_op jit(solution)/shard_map/ppermute | solution.py:338
